TPU v7x, 1024 devices: a whole 8x8x8 slice. The times are simulated.
1024 devices in a mesh: dp: 32 (over y, x_lo, core), blk: 32 (over z, x_hi).
Axes of the slice: x: 8 (x_hi: 4, x_lo: 2; x = x_hi * 2 + x_lo), y: 8, z: 8, core: 2. Of those that a mesh axis runs over, the one named last changes fastest.
Arguments:
- captions: bfloat16 [16384, 1152], P('dp'), may hold values from -6 to 6
- w_in: bfloat16 [1152, 4096], P(None, 'blk'), may hold values from -0.1875 to 0.1875
- w_out: bfloat16 [4096, 1152], P('blk'), may hold values from -0.09375 to 0.09375
- images: bfloat16 [1024, 1152], P('blk'), may hold values from -6 to 6
- pairs: int32 [16384], P('dp'), may hold values from 0 to 1023
Outputs:
- grad_w_in: float32 [1152, 4096], P('dp', 'blk')
- grad_w_out_t: float32 [1152, 4096], P('dp', 'blk')
All inputs are finite; a program needn't handle non-finite values.
Results may differ from a plain program's by a relative error of at most 0.005.
Values may be sent and summed in bfloat16 or wider, within the bound.
No kernel may reach another device: no remote copies, remote signals or barrier semaphores. Data moves between devices by JAX's collectives and lax.ppermute only.
A program may use at most 32 MiB of HBM per device.

v0:
```python
import jax
import jax.numpy as jnp
from jax import lax
from jax.sharding import Mesh
from jax.sharding import PartitionSpec as P

BLK = ("blk_0", "blk_1")


SCORE_SCALE = 10.0
SCORE_BIAS_TERM = -5.0
EPSILON = 1e-06


def own_rows_2(total, axes):
    for axis in axes:
        total = lax.psum_scatter(total, axis, scatter_dimension=0, tiled=True)
    return total


def sum_by_axis(x, axes, dim):
    for axis in axes:
        x = lax.psum_scatter(x, axis, scatter_dimension=dim, tiled=True)
    return x


def sent_to_all(x, axis):
    peers = lax.axis_size(axis)
    return lax.all_to_all(jnp.broadcast_to(x[None], (peers, *x.shape)), axis, 0, 0, tiled=True)


def joined_along(tiles, dim):
    shape = list(tiles.shape[1:])
    shape[dim] *= tiles.shape[0]
    return jnp.moveaxis(tiles, 0, dim).reshape(shape)


def gather_directly(x, axis, dim):
    tiles = sent_to_all(x, axis)
    return joined_along(tiles, dim)


def split_up(x, dim, peers):
    shape = x.shape
    tiles = x.reshape(*shape[:dim], peers, shape[dim] // peers, *shape[dim + 1 :])
    return jnp.moveaxis(tiles, dim, 0)


def sum_together(arrays, axis, dims):
    peers = lax.axis_size(axis)
    tiles = [split_up(a, dim, peers) for a, dim in zip(arrays, dims)]
    lines = jnp.concatenate([b.reshape(peers, -1) for b in tiles], axis=1)
    extent = max(16, -(-lines.shape[1] // 1024) * 8)
    lines = jnp.pad(lines, ((0, 0), (0, extent * 128 - lines.shape[1]))).reshape(-1, 128)
    ravelled, at, done = (lax.psum_scatter(lines, axis, tiled=True).reshape(-1), 0, [])
    for b in tiles:
        part = b[0]
        done.append(ravelled[at : at + part.size].reshape(part.shape))
        at += part.size
    return tuple(done)


def activate(values):
    return jax.nn.gelu(values, approximate=True)


def tile_grad(direction_halfway, image_direction, first_image, row_pairs):
    pair_scores = (
        SCORE_SCALE
        * lax.dot_general(
            direction_halfway,
            image_direction,
            (((1,), (1,)), ((), ())),
            preferred_element_type=jnp.float32,
        )
        + SCORE_BIAS_TERM
    )
    columns = first_image + lax.broadcasted_iota(jnp.int32, pair_scores.shape, 1)
    labels = (row_pairs[:, None] == columns).astype(jnp.float32)
    label_error = (jax.nn.sigmoid(pair_scores) - labels).astype(jnp.bfloat16)
    return SCORE_SCALE * jnp.dot(label_error, image_direction, preferred_element_type=jnp.float32)


def body(captions, w_in, w_out, images, pairs):
    cycle_pos = lax.axis_index(BLK)
    block_len = images.shape[0]
    pre_act = jnp.dot(captions, w_in, preferred_element_type=jnp.float32)
    hidden = activate(pre_act).astype(jnp.bfloat16)
    rows_hidden = hidden
    embedding = own_rows_2(jnp.dot(rows_hidden, w_out, preferred_element_type=jnp.float32), BLK)
    inv_norm = lax.rsqrt(jnp.sum(embedding * embedding, axis=1, keepdims=True) + EPSILON)
    unit_dir = embedding * inv_norm
    direction_halfway = unit_dir.astype(jnp.bfloat16)
    image_vals = images.astype(jnp.float32)
    image_direction = (
        image_vals * lax.rsqrt(jnp.sum(image_vals * image_vals, axis=1, keepdims=True) + EPSILON)
    ).astype(jnp.bfloat16)
    first_local = cycle_pos * block_len
    partial_grads = tile_grad(
        lax.all_gather(direction_halfway, BLK, axis=0, tiled=True),
        image_direction,
        first_local,
        pairs,
    )
    direction_gradient = sum_by_axis(partial_grads, BLK, 0)
    embed_grad = (
        direction_gradient
        - unit_dir * jnp.sum(unit_dir * direction_gradient, axis=1, keepdims=True)
    ) * inv_norm
    embed_half = embed_grad.astype(jnp.bfloat16)
    piece = gather_directly(embed_half, BLK, 0)
    rows_hidden = hidden
    hidden_grad = lax.dot_general(
        piece, w_out, (((1,), (1,)), ((), ())), preferred_element_type=jnp.float32
    )
    _, pullback = jax.vjp(activate, pre_act)
    preact_grad = pullback(hidden_grad)[0].astype(jnp.bfloat16)
    grad_in = lax.dot_general(
        captions, preact_grad, (((0,), (0,)), ((), ())), preferred_element_type=jnp.float32
    )
    grad_out = lax.dot_general(
        piece, rows_hidden, (((0,), (0,)), ((), ())), preferred_element_type=jnp.float32
    )
    grad_in, grad_out = (grad_in, grad_out)
    grad_w_in, grad_w_out_t = sum_together((grad_in, grad_out), "dp", (0, 0))
    return (grad_w_in, grad_w_out_t)


def solution(mesh):
    finer = Mesh(mesh.devices.reshape(mesh.shape["dp"], 8, 4), ("dp", "blk_0", "blk_1"))
    placed = (P("dp", None), P(None, BLK), P(BLK, None), P(BLK, None), P("dp"))
    return jax.shard_map(
        body, mesh=finer, in_specs=placed, out_specs=(P("dp", BLK), P("dp", BLK)), check_vma=False
    )
```

profile of v0, /device:TPU:1, one launch (start us, length us, event | category | flops | bytes accessed | tf_op | source)
XLA Modules:
  0.0 582.3 jit_solution(10474256165073226735)
XLA Ops:
  7.2 0.0 reduce-scatter.5.cloned.1.call-start
  7.2 1.2 copy-done
  8.4 1.4 fusion.47
  9.9 1.9 fusion.44
  11.8 0.0 reduce-scatter.7.cloned.1.call-start
  11.8 58.6 %reduce-scatter.5.cloned.1.call-done = f32[64,1152]{1,0:T(8,128)} async-done(((f32[512,1152]{1,0:T(8,128)}), f32[64,1152]{1,0:T(8,128)}) %reduce-scatter.5.cloned.1.call-update) | async-done | bytes 294928 | tf_op jit(solution)/shard_map/reduce_scatter | solution.py:17
  70.5 0.0 all-gather.2.cloned.1.call-start
  70.5 34.0 %reduce-scatter.7.cloned.1.call-done = f32[16,1152]{1,0:T(8,128)} async-done(((f32[64,1152]{1,0:T(8,128)}), f32[16,1152]{1,0:T(8,128)}) %reduce-scatter.7.cloned.1.call-update) | async-done | bytes 73744 | tf_op jit(solution)/shard_map/reduce_scatter | solution.py:17
  104.5 1.0 multiply_reduce_fusion.1
  105.6 1.6 multiply_convert_fusion.2
  107.2 0.0 reduce-scatter.9.cloned.1.call-start
  107.2 0.1 fusion.14
  107.4 88.8 %all-gather.2.cloned.1.call-done = bf16[512,1152]{1,0:T(8,128)(2,1)} async-done(((bf16[16,1152]{1,0:T(8,128)(2,1)}), bf16[512,1152]{1,0:T(8,128)(2,1)}) %all-gather.2.cloned.1.call-update) | async-done | bytes 1179664 | tf_op jit(solution)/shard_map/all_gather | solution.py:100
  196.2 3.7 convolution_multiply_fusion
  199.9 0.0 reduce-scatter.11.cloned.1.call-start
  200.0 46.9 %reduce-scatter.9.cloned.1.call-done = f32[64,1152]{1,0:T(8,128)} async-done(((f32[512,1152]{1,0:T(8,128)}), f32[64,1152]{1,0:T(8,128)}) %reduce-scatter.9.cloned.1.call-update) | async-done | bytes 294928 | tf_op jit(solution)/shard_map/reduce_scatter | solution.py:23
  246.9 0.0 all-reduce.3.cloned.1.call-start
  246.9 34.1 %reduce-scatter.11.cloned.1.call-done = f32[16,1152]{1,0:T(8,128)} async-done(((f32[64,1152]{1,0:T(8,128)}), f32[16,1152]{1,0:T(8,128)}) %reduce-scatter.11.cloned.1.call-update) | async-done | bytes 73744 | tf_op jit(solution)/shard_map/reduce_scatter | solution.py:23
  281.1 1.1 multiply_reduce_fusion
  282.2 1.0 multiply_convert_fusion.1
  283.1 0.1 broadcast_in_dim.2
  283.2 41.3 %all_to_all.5 = bf16[32,16,1152]{2,1,0:T(8,128)(2,1)S(1)} all-to-all(bf16[32,16,1152]{2,1,0:T(8,128)(2,1)S(1)} %broadcast_in_dim.2), channel_id=1, replica_groups=mesh['dp'=32,'blk_0'=8,'blk_1'=4] {'blk_0','blk_1'}, dimensions={0} | all-to-all | bytes 2359296 | tf_op jit(solution)/shard_map/all_to_all | solution.py:29
  324.5 1.9 convolution_bitcast_fusion
  326.4 0.5 fusion.43
  326.9 1.3 copy.8
  328.2 0.9 reshape_reshape.6
  329.1 0.9 reshape_reshape.7
  330.1 1.3 pad_maximum_fusion
  331.4 1.2 reshape.33
  332.6 1.3 dynamic-slice
  334.6 239.5 %all-reduce.3.cloned.1.call-done = f32[2304,128]{1,0:T(8,128)} async-done(((f32[2304,128]{1,0:T(8,128)}), f32[2304,128]{1,0:T(8,128)}) %all-reduce.3.cloned.1.call-update) | async-done | bytes 1179664
  574.1 1.4 constant_dynamic-slice_fusion.1
  (18 shorter events, 0.1 us)
Async XLA Ops:
  7.2 1.3 copy-start
  7.2 2.7 copy-start.2
  7.2 63.3 %reduce-scatter.5.cloned.1.call-start = ((), (), s32[]{:S(2)}) async-start(), calls=%async_computation.5 | async-start | bytes 2654208 | tf_op jit(solution)/shard_map/reduce_scatter | solution.py:17
  11.8 95.5 %copy-start.3 = (bf16[32,1152]{1,0:T(8,128)(2,1)S(1)}, bf16[32,1152]{1,0:T(8,128)(2,1)}, u32[]{:S(2)}) copy-start(bf16[32,1152]{1,0:T(8,128)(2,1)} %param.8) | copy-start | bytes 221188
  11.8 184.4 %copy-start.4 = (s32[512]{0:T(512)S(1)}, s32[512]{0:T(512)}, u32[]{:S(2)}) copy-start(s32[512]{0:T(512)} %param.9) | copy-start | bytes 6148
  11.8 92.7 %reduce-scatter.7.cloned.1.call-start = ((), (), s32[]{:S(2)}) async-start(), calls=%async_computation.6 | async-start | bytes 368640 | tf_op jit(solution)/shard_map/reduce_scatter | solution.py:17
  70.5 125.7 %all-gather.2.cloned.1.call-start = ((), (), s32[]{:S(2)}) async-start(), calls=%async_computation.7 | async-start | bytes 1216512 | tf_op jit(solution)/shard_map/all_gather | solution.py:100
  107.2 139.7 %reduce-scatter.9.cloned.1.call-start = ((), (), s32[]{:S(2)}) async-start(), calls=%async_computation.8 | async-start | bytes 2654208 | tf_op jit(solution)/shard_map/reduce_scatter | solution.py:23
  199.9 81.2 %copy-start.1 = (f32[16,1152]{1,0:T(8,128)S(1)}, f32[16,1152]{1,0:T(8,128)}, u32[]{:S(2)}) copy-start(f32[16,1152]{1,0:T(8,128)} %reduce-scatter.7.cloned.1.call-done) | copy-start | bytes 221188
  199.9 81.1 %reduce-scatter.11.cloned.1.call-start = ((), (), s32[]{:S(2)}) async-start(), calls=%async_computation.9 | async-start | bytes 368640 | tf_op jit(solution)/shard_map/reduce_scatter | solution.py:23
  246.9 327.2 %all-reduce.3.cloned.1.call-start = ((), (), s32[]{:S(2)}) async-start(), calls=%async_computation.10 | async-start | bytes 2359296
Sparse Core Ops, SparseCore 0:
  11.9 58.4 reduce-scatter.4
  73.9 30.6 reduce-scatter.6
  108.9 87.2 all-gather.1
  200.1 46.7 reduce-scatter.8
  250.1 30.9 reduce-scatter.10
  332.8 241.2 all-reduce.2
where the time goes:
time: 583 us; the launch traced here: 582 us
  waiting for transfers between devices  502 us (86%)
  blocking collectives  41.3 us (7%)
  between operations  14.8 us (3%)
  matrix products  9.42 us (2%)
  local copies, waits for them, and re-layouts  8.39 us (1%)
  other arithmetic  6.09 us (1%)
    unnamed x7, waiting for transfers between devices  240 us
    reduce_scatter x2, waiting for transfers between devices, own_rows_2(): total = lax.psum_scatter(total, axis, scatter_dimension=0, tiled=True)  92.6 us
    all_gather x1, waiting for transfers between devices, body(): lax.all_gather(direction_halfway, BLK, axis=0, tiled=True)  88.8 us
    reduce_scatter x2, waiting for transfers between devices, sum_by_axis(): x = lax.psum_scatter(x, axis, scatter_dimension=dim, tiled=True)  81 us
    all_to_all x1, blocking collectives, sent_to_all(): lax.all_to_all(jnp.broadcast_to(x[None], (peers, *x.shape)), axis, 0, 0,...  41.3 us
  transfers between devices with their start and end apart: 6, of which 6 were waited for; matrix products, arithmetic and copies ran while one was open for 0% of the time, Pallas kernels for 0%

commit v1 on v0

v1 whole, which is shorter than its diff:
```python
import jax
import jax.numpy as jnp
from jax import lax
from jax.sharding import Mesh
from jax.sharding import PartitionSpec as P

DP = ("y", "xl", "core")
BLK = ("z", "xh")
PAIR = ("xl", "core")

SCALE = 10.0
BIAS = -5.0
EPS = 1e-06
BF16 = jnp.bfloat16
F32 = jnp.float32


def exchange(x, axes):
    return lax.all_to_all(x, axes, 0, 0, tiled=True)


def to_all(x, n):
    return jnp.broadcast_to(x[None], (n, *x.shape))


def activate(values):
    return jax.nn.gelu(values, approximate=True)


def body(captions, w_in, w_out, images, pairs):
    rows, width = captions.shape
    n_z, n_xh, n_y = lax.axis_size("z"), lax.axis_size("xh"), lax.axis_size("y")
    n_c = lax.axis_size("xl") * lax.axis_size("core")
    n_dp = n_y * n_c
    per_xh = rows // n_xh
    own = per_xh // n_z
    img_block = images.shape[0]
    img_part = img_block // n_c
    c = lax.axis_index(PAIR)

    img = lax.dynamic_slice_in_dim(images, c * img_part, img_part, 0).astype(F32)
    img = (img * lax.rsqrt(jnp.sum(img * img, axis=1, keepdims=True) + EPS)).astype(BF16)

    pre_act = jnp.dot(captions, w_in, preferred_element_type=F32)
    hidden = activate(pre_act).astype(BF16)
    partial = jnp.dot(hidden, w_out, preferred_element_type=F32).astype(BF16)

    sent = jnp.concatenate([partial.reshape(n_xh, per_xh, width), to_all(img, n_xh)], axis=1)
    got = exchange(sent, "xh")
    partial = jnp.sum(got[:, :per_xh].astype(F32), axis=0).astype(BF16)
    img = got[:, per_xh:].reshape(n_xh * img_part, width)
    sent = jnp.concatenate([partial.reshape(n_z, own, width), to_all(img, n_z)], axis=1)
    got = exchange(sent, "z")
    embedding = jnp.sum(got[:, :own].astype(F32), axis=0)
    img = got[:, own:].reshape(-1, width)
    n_img = img.shape[0]

    inv_norm = lax.rsqrt(jnp.sum(embedding * embedding, axis=1, keepdims=True) + EPS)
    unit_dir = embedding * inv_norm

    first = lax.axis_index("xh") * per_xh + lax.axis_index("z") * own
    pair = lax.dynamic_slice_in_dim(pairs, first, own, 0)[:, None]
    lane = lax.broadcasted_iota(jnp.int32, (own, 128), 1)
    digits = jnp.where(lane == 0, pair // 32, jnp.where(lane == 1, pair % 32, 0)).astype(BF16)
    got = exchange(to_all(jnp.concatenate([unit_dir.astype(BF16), digits], axis=1), n_c), PAIR)
    got = got.reshape(n_c * own, width + 128)
    unit_half = got[:, :width]
    pair = (got[:, width : width + 1].astype(F32) * 32 + got[:, width + 1 : width + 2].astype(F32)).astype(jnp.int32)

    logits = (
        SCALE * lax.dot_general(unit_half, img, (((1,), (1,)), ((), ())), preferred_element_type=F32) + BIAS
    )
    n = lax.broadcasted_iota(jnp.int32, (1, n_img), 1)
    column = (n // img_part) * img_block + c * img_part + n % img_part
    label = (pair == column).astype(F32)
    mismatch = (jax.nn.sigmoid(logits) - label).astype(BF16)
    grad = SCALE * jnp.dot(mismatch, img, preferred_element_type=F32)
    unit_grad = jnp.sum(exchange(grad.reshape(n_c, own, width), PAIR), axis=0)

    embed_half = (
        (unit_grad - unit_dir * jnp.sum(unit_dir * unit_grad, axis=1, keepdims=True)) * inv_norm
    ).astype(BF16)
    got = exchange(to_all(embed_half, n_z), "z").reshape(per_xh, width)
    embed_half = exchange(to_all(got, n_xh), "xh").reshape(rows, width)

    hidden_grad = lax.dot_general(embed_half, w_out, (((1,), (1,)), ((), ())), preferred_element_type=F32)
    _, pullback = jax.vjp(activate, pre_act)
    preact_grad = pullback(hidden_grad)[0].astype(BF16)
    grad_in = lax.dot_general(captions, preact_grad, (((0,), (0,)), ((), ())), preferred_element_type=F32)
    grad_out = lax.dot_general(embed_half, hidden, (((0,), (0,)), ((), ())), preferred_element_type=F32)
    share = width // n_dp
    sent = jnp.concatenate(
        [grad_in.astype(BF16).reshape(n_dp, share, -1), grad_out.astype(BF16).reshape(n_dp, share, -1)], axis=1
    )
    total = jnp.sum(exchange(sent, DP).astype(F32), axis=0)
    return total[:share], total[share:]


def solution(mesh):
    fine = Mesh(mesh.devices.reshape(8, 2, 2, 8, 4), (*DP, *BLK))
    placed = (P(DP, None), P(None, BLK), P(BLK, None), P(BLK, None), P(DP))
    return jax.shard_map(
        body, mesh=fine, in_specs=placed, out_specs=(P(DP, BLK), P(DP, BLK)), check_vma=False
    )
```

time: 583 us -> 198 us (0.34)
  waiting for transfers between devices: 502 us -> 26.7 us
  blocking collectives: 41.3 us -> 137 us
  starting transfers between devices: 0.24 us -> 22.5 us
  between operations: 14.8 us -> 0.8 us
  local copies, waits for them, and re-layouts: 8.39 us -> 1.85 us
    unnamed x7 -> x0, waiting for transfers between devices: 240 us -> none
    reduce_scatter x4 -> x0, waiting for transfers between devices: 174 us -> none  [the longest x2 92.6 us: own_rows_2(): total = lax.psum_scatter(total, axis, scatter_dimension=0, tiled=True)]
    all_to_all x1 -> x5, blocking collectives: 41.3 us -> 137 us  [exchange(): return lax.all_to_all(x, axes, 0, 0, tiled=True)]
    all_gather x1 -> x0, waiting for transfers between devices: 88.8 us -> none  [body(): lax.all_gather(direction_halfway, BLK, axis=0, tiled=True)]
    all_to_all x0 -> x2, waiting for transfers between devices: none -> 26.7 us  [exchange(): return lax.all_to_all(x, axes, 0, 0, tiled=True)]
    all_to_all x0 -> x2, starting transfers between devices: none -> 22.5 us  [exchange(): return lax.all_to_all(x, axes, 0, 0, tiled=True)]
  transfers between devices with their start and end apart: 6 -> 2, of which waited for: 6 -> 2; matrix products, arithmetic and copies ran while one was open for 0% -> 0% of each run, Pallas kernels for 0% -> 0%
where the time goes in v1:
time: 198 us
  blocking collectives  137 us (69%)
  waiting for transfers between devices  26.7 us (13%)
  starting transfers between devices  22.5 us (11%)
  other arithmetic  4.84 us (2%)
  matrix products  4.19 us (2%)
    all_to_all x5, blocking collectives, exchange(): return lax.all_to_all(x, axes, 0, 0, tiled=True)  137 us
    all_to_all x2, waiting for transfers between devices, exchange(): return lax.all_to_all(x, axes, 0, 0, tiled=True)  26.7 us
    all_to_all x2, starting transfers between devices, exchange(): return lax.all_to_all(x, axes, 0, 0, tiled=True)  22.5 us
  transfers between devices with their start and end apart: 2, of which 2 were waited for; matrix products, arithmetic and copies ran while one was open for 0% of the time, Pallas kernels for 0%

profile of v1, /device:TPU:1, one launch (start us, length us, event | category | flops | bytes accessed | tf_op | source)
XLA Modules:
  0.0 197.8 jit_solution(8507265474118217148)
XLA Ops:
  0.7 1.0 fusion.26
  1.6 0.8 fusion.27
  2.4 1.4 fusion.50
  3.9 0.5 convolution_convert_fusion
  4.4 0.1 pad_maximum_fusion
  4.5 37.5 %all_to_all.35 = bf16[4,136,1152]{2,1,0:T(8,128)(2,1)S(1)} all-to-all(bf16[4,136,1152]{2,1,0:T(8,128)(2,1)S(1)} %pad_maximum_fusion), channel_id=1, replica_groups=mesh['y'=8,'xl'=2,'core'=2,'z'=8,'xh'=4] {'xh'}, dimensions={0} | all-to-all | bytes 2506752 | tf_op jit(solution)/shard_map/all_to_all | solution.py:19
  42.0 0.2 slice_reduce_fusion
  42.2 1.0 pad_maximum_fusion.1
  43.2 16.8 %all-to-all-start.1 = ((bf16[8,48,1152]{2,1,0:T(8,128)(2,1)}), bf16[8,48,1152]{2,1,0:T(8,128)(2,1)S(1)}, u32[]{:S(2)}, u32[]{:S(2)}) async-start(bf16[8,48,1152]{2,1,0:T(8,128)(2,1)} %pad_maximum_fusion.1), calls=%async_computation.1 | async-start | bytes 1769472 | tf_op jit(solution)/shard_map/all_to_all | solution.py:19
  60.0 0.8 and_select_fusion.3
  60.8 0.1 select_convert_fusion
  60.8 22.9 %all-to-all-done.1 = bf16[8,48,1152]{2,1,0:T(8,128)(2,1)S(1)} async-done(((bf16[8,48,1152]{2,1,0:T(8,128)(2,1)}), bf16[8,48,1152]{2,1,0:T(8,128)(2,1)S(1)}, u32[]{:S(2)}, u32[]{:S(2)}) %all-to-all-start.1) | async-done | bytes 884768 | tf_op jit(solution)/shard_map/all_to_all | solution.py:19
  83.8 0.1 multiply_reduce_fusion.1
  83.9 0.1 multiply_convert_fusion.2
  84.0 0.7 broadcast_in_dim.59
  84.7 5.7 %all-to-all-start.2 = ((bf16[4,16,1280]{2,1,0:T(8,128)(2,1)}), bf16[4,16,1280]{2,1,0:T(8,128)(2,1)S(1)}, u32[]{:S(2)}, u32[]{:S(2)}) async-start(bf16[4,16,1280]{2,1,0:T(8,128)(2,1)} %broadcast_in_dim.59), calls=%async_computation.2 | async-start | bytes 327680 | tf_op jit(solution)/shard_map/all_to_all | solution.py:19
  90.4 3.8 %all-to-all-done.2 = bf16[4,16,1280]{2,1,0:T(8,128)(2,1)S(1)} async-done(((bf16[4,16,1280]{2,1,0:T(8,128)(2,1)}), bf16[4,16,1280]{2,1,0:T(8,128)(2,1)S(1)}, u32[]{:S(2)}, u32[]{:S(2)}) %all-to-all-start.2) | async-done | bytes 163872 | tf_op jit(solution)/shard_map/all_to_all | solution.py:19
  94.2 0.2 convert_reduce_fusion.2
  94.4 0.6 convolution_multiply_fusion
  95.1 9.3 %all_to_all.36 = f32[4,16,1152]{2,1,0:T(8,128)S(1)} all-to-all(f32[4,16,1152]{2,1,0:T(8,128)S(1)} %bitcast.25), channel_id=1, replica_groups=mesh['y'=8,'xl'=2,'core'=2,'z'=8,'xh'=4] {'xl','core'}, dimensions={0} | all-to-all | bytes 589824 | tf_op jit(solution)/shard_map/all_to_all | solution.py:19
  104.4 0.2 multiply_reduce_fusion
  104.5 0.1 multiply_convert_fusion.1
  104.7 14.7 %all_to_all.37 = bf16[8,16,1152]{2,1,0:T(8,128)(2,1)S(1)} all-to-all(bf16[8,16,1152]{2,1,0:T(8,128)(2,1)S(1)} %broadcast_in_dim.60), channel_id=1, replica_groups=mesh['y'=8,'xl'=2,'core'=2,'z'=8,'xh'=4] {'z'}, dimensions={0} | all-to-all | bytes 589824 | tf_op jit(solution)/shard_map/all_to_all | solution.py:19
  119.4 0.1 broadcast_in_dim.62
  119.5 32.9 %all_to_all.38 = bf16[4,128,1152]{2,1,0:T(8,128)(2,1)S(1)} all-to-all(bf16[4,128,1152]{2,1,0:T(8,128)(2,1)S(1)} %broadcast_in_dim.62), channel_id=1, replica_groups=mesh['y'=8,'xl'=2,'core'=2,'z'=8,'xh'=4] {'xh'}, dimensions={0} | all-to-all | bytes 2359296 | tf_op jit(solution)/shard_map/all_to_all | solution.py:19
  152.3 1.1 fusion
  153.4 0.6 convolution_convert_fusion.1
  154.0 0.2 copy.11
  154.3 0.1 pad_maximum_fusion.2
  154.5 42.6 %all_to_all.39 = bf16[32,72,128]{2,1,0:T(8,128)(2,1)S(1)} all-to-all(bf16[32,72,128]{2,1,0:T(8,128)(2,1)S(1)} %pad_maximum_fusion.2), channel_id=1, replica_groups=mesh['y'=8,'xl'=2,'core'=2,'z'=8,'xh'=4] {'y','xl','core'}, dimensions={0} | all-to-all | bytes 1179648 | tf_op jit(solution)/shard_map/all_to_all | solution.py:19
  197.1 0.1 convert_reduce_fusion
  197.2 0.6 fusion.47
  (21 shorter events, 0.4 us)
Async XLA Ops:
  0.6 1.8 copy-start
  0.6 3.2 %copy-start.1 = (bf16[128,1152]{1,0:T(8,128)(2,1)S(1)}, bf16[128,1152]{1,0:T(8,128)(2,1)}, u32[]{:S(2)}) copy-start(bf16[128,1152]{1,0:T(8,128)(2,1)} %param.7) | copy-start | bytes 884740
  43.2 40.5 %all-to-all-start.1 = ((bf16[8,48,1152]{2,1,0:T(8,128)(2,1)}), bf16[8,48,1152]{2,1,0:T(8,128)(2,1)S(1)}, u32[]{:S(2)}, u32[]{:S(2)}) async-start(bf16[8,48,1152]{2,1,0:T(8,128)(2,1)} %pad_maximum_fusion.1), calls=%async_computation.1 | async-start | bytes 1769472 | tf_op jit(solution)/shard_map/all_to_all | solution.py:19
  84.7 9.6 %all-to-all-start.2 = ((bf16[4,16,1280]{2,1,0:T(8,128)(2,1)}), bf16[4,16,1280]{2,1,0:T(8,128)(2,1)S(1)}, u32[]{:S(2)}, u32[]{:S(2)}) async-start(bf16[4,16,1280]{2,1,0:T(8,128)(2,1)} %broadcast_in_dim.59), calls=%async_computation.2 | async-start | bytes 327680 | tf_op jit(solution)/shard_map/all_to_all | solution.py:19
  119.5 32.9 %copy-start.2 = (bf16[128,1152]{1,0:T(8,128)(2,1)S(1)}, bf16[128,1152]{1,0:T(8,128)(2,1)}, u32[]{:S(2)}) copy-start(bf16[128,1152]{1,0:T(8,128)(2,1)} %param.7) | copy-start | bytes 884740

commit v2 on v1

--- a/solution.py
+++ b/solution.py
@@ -29,11 +29,8 @@
 
 def body(captions, w_in, w_out, images, pairs):
     rows, width = captions.shape
-    n_z, n_xh, n_y = lax.axis_size("z"), lax.axis_size("xh"), lax.axis_size("y")
-    n_c = lax.axis_size("xl") * lax.axis_size("core")
-    n_dp = n_y * n_c
-    per_xh = rows // n_xh
-    own = per_xh // n_z
+    n_blk, n_dp, n_c = lax.axis_size(BLK), lax.axis_size(DP), lax.axis_size(PAIR)
+    own = rows // n_blk
     img_block = images.shape[0]
     img_part = img_block // n_c
     c = lax.axis_index(PAIR)
@@ -45,12 +42,8 @@
     hidden = activate(pre_act).astype(BF16)
     partial = jnp.dot(hidden, w_out, preferred_element_type=F32).astype(BF16)
 
-    sent = jnp.concatenate([partial.reshape(n_xh, per_xh, width), to_all(img, n_xh)], axis=1)
-    got = exchange(sent, "xh")
-    partial = jnp.sum(got[:, :per_xh].astype(F32), axis=0).astype(BF16)
-    img = got[:, per_xh:].reshape(n_xh * img_part, width)
-    sent = jnp.concatenate([partial.reshape(n_z, own, width), to_all(img, n_z)], axis=1)
-    got = exchange(sent, "z")
+    sent = jnp.concatenate([partial.reshape(n_blk, own, width), to_all(img, n_blk)], axis=1)
+    got = exchange(sent, BLK)
     embedding = jnp.sum(got[:, :own].astype(F32), axis=0)
     img = got[:, own:].reshape(-1, width)
     n_img = img.shape[0]
@@ -58,8 +51,7 @@
     inv_norm = lax.rsqrt(jnp.sum(embedding * embedding, axis=1, keepdims=True) + EPS)
     unit_dir = embedding * inv_norm
 
-    first = lax.axis_index("xh") * per_xh + lax.axis_index("z") * own
-    pair = lax.dynamic_slice_in_dim(pairs, first, own, 0)[:, None]
+    pair = lax.dynamic_slice_in_dim(pairs, lax.axis_index(BLK) * own, own, 0)[:, None]
     lane = lax.broadcasted_iota(jnp.int32, (own, 128), 1)
     digits = jnp.where(lane == 0, pair // 32, jnp.where(lane == 1, pair % 32, 0)).astype(BF16)
     got = exchange(to_all(jnp.concatenate([unit_dir.astype(BF16), digits], axis=1), n_c), PAIR)
@@ -80,8 +72,7 @@
     embed_half = (
         (unit_grad - unit_dir * jnp.sum(unit_dir * unit_grad, axis=1, keepdims=True)) * inv_norm
     ).astype(BF16)
-    got = exchange(to_all(embed_half, n_z), "z").reshape(per_xh, width)
-    embed_half = exchange(to_all(got, n_xh), "xh").reshape(rows, width)
+    embed_half = exchange(to_all(embed_half, n_blk), BLK).reshape(rows, width)
 
     hidden_grad = lax.dot_general(embed_half, w_out, (((1,), (1,)), ((), ())), preferred_element_type=F32)
     _, pullback = jax.vjp(activate, pre_act)

time: 198 us -> 176 us (0.89)
  blocking collectives: 137 us -> 78.8 us
  waiting for transfers between devices: 26.7 us -> 54.8 us
  starting transfers between devices: 22.5 us -> 29.2 us
    all_to_all x5 -> x3, blocking collectives: 137 us -> 78.8 us  [exchange(): return lax.all_to_all(x, axes, 0, 0, tiled=True)]
    all_to_all x2, waiting for transfers between devices: 26.7 us -> 54.8 us  [exchange(): return lax.all_to_all(x, axes, 0, 0, tiled=True)]
    all_to_all x2, starting transfers between devices: 22.5 us -> 29.2 us  [exchange(): return lax.all_to_all(x, axes, 0, 0, tiled=True)]
where the time goes in v2:
time: 176 us; the launch traced here: 175 us
  blocking collectives  78.8 us (45%)
  waiting for transfers between devices  54.8 us (31%)
  starting transfers between devices  29.2 us (17%)
  other arithmetic  5.06 us (3%)
  matrix products  4.88 us (3%)
  local copies, waits for them, and re-layouts  1.76 us (1%)
    all_to_all x3, blocking collectives, exchange(): return lax.all_to_all(x, axes, 0, 0, tiled=True)  78.8 us
    all_to_all x2, waiting for transfers between devices, exchange(): return lax.all_to_all(x, axes, 0, 0, tiled=True)  54.8 us
    all_to_all x2, starting transfers between devices, exchange(): return lax.all_to_all(x, axes, 0, 0, tiled=True)  29.2 us
  transfers between devices with their start and end apart: 2, of which 2 were waited for; matrix products, arithmetic and copies ran while one was open for 0% of the time, Pallas kernels for 0%

profile of v2, /device:TPU:1, one launch (start us, length us, event | category | flops | bytes accessed | tf_op | source)
XLA Modules:
  0.0 175.2 jit_solution(18234613644302130374)
XLA Ops:
  0.6 0.0 copy-start
  0.7 1.0 fusion.26
  1.6 0.8 fusion.27
  2.4 1.4 fusion.50
  3.9 0.5 convolution_convert_fusion
  4.4 1.4 pad_maximum_fusion
  5.8 22.5 %all-to-all-start = ((bf16[32,24,1152]{2,1,0:T(8,128)(2,1)}), bf16[32,24,1152]{2,1,0:T(8,128)(2,1)S(1)}, u32[]{:S(2)}, u32[]{:S(2)}) async-start(bf16[32,24,1152]{2,1,0:T(8,128)(2,1)} %pad_maximum_fusion), calls=%async_computation | async-start | bytes 3538944 | tf_op jit(solution)/shard_map/all_to_all | solution.py:19
  28.3 0.8 and_select_fusion.3
  29.1 0.1 select_convert_fusion
  29.2 50.9 %all-to-all-done = bf16[32,24,1152]{2,1,0:T(8,128)(2,1)S(1)} async-done(((bf16[32,24,1152]{2,1,0:T(8,128)(2,1)}), bf16[32,24,1152]{2,1,0:T(8,128)(2,1)S(1)}, u32[]{:S(2)}, u32[]{:S(2)}) %all-to-all-start) | async-done | bytes 1769504 | tf_op jit(solution)/shard_map/all_to_all | solution.py:19
  80.1 0.2 convert_reduce_fusion
  80.3 0.1 multiply_reduce_fusion.1
  80.4 0.1 multiply_convert_fusion.2
  80.5 0.7 broadcast_in_dim.27
  81.2 6.6 %all-to-all-start.1 = ((bf16[4,16,1280]{2,1,0:T(8,128)(2,1)}), bf16[4,16,1280]{2,1,0:T(8,128)(2,1)S(1)}, u32[]{:S(2)}, u32[]{:S(2)}) async-start(bf16[4,16,1280]{2,1,0:T(8,128)(2,1)} %broadcast_in_dim.27), calls=%async_computation.1 | async-start | bytes 327680 | tf_op jit(solution)/shard_map/all_to_all | solution.py:19
  87.8 3.8 %all-to-all-done.1 = bf16[4,16,1280]{2,1,0:T(8,128)(2,1)S(1)} async-done(((bf16[4,16,1280]{2,1,0:T(8,128)(2,1)}), bf16[4,16,1280]{2,1,0:T(8,128)(2,1)S(1)}, u32[]{:S(2)}, u32[]{:S(2)}) %all-to-all-start.1) | async-done | bytes 163872 | tf_op jit(solution)/shard_map/all_to_all | solution.py:19
  91.6 0.2 convert_reduce_fusion.2
  91.8 1.4 convolution_multiply_fusion
  93.2 10.3 %all_to_all.25 = f32[4,16,1152]{2,1,0:T(8,128)S(1)} all-to-all(f32[4,16,1152]{2,1,0:T(8,128)} %bitcast.20), channel_id=1, replica_groups=mesh['y'=8,'xl'=2,'core'=2,'z'=8,'xh'=4] {'xl','core'}, dimensions={0} | all-to-all | bytes 589824 | tf_op jit(solution)/shard_map/all_to_all | solution.py:19
  103.5 0.2 multiply_reduce_fusion
  103.7 0.1 multiply_convert_fusion.1
  103.8 0.1 broadcast_in_dim.28
  103.9 42.0 %all_to_all.26 = bf16[32,16,1152]{2,1,0:T(8,128)(2,1)S(1)} all-to-all(bf16[32,16,1152]{2,1,0:T(8,128)(2,1)S(1)} %broadcast_in_dim.28), channel_id=1, replica_groups=mesh['y'=8,'xl'=2,'core'=2,'z'=8,'xh'=4] {'z','xh'}, dimensions={0} | all-to-all | bytes 2359296 | tf_op jit(solution)/shard_map/all_to_all | solution.py:19
  145.9 1.1 fusion
  147.0 0.6 convolution_convert_fusion.1
  147.6 0.2 copy.10
  147.8 0.1 reshape.171
  147.8 0.1 reshape.172
  147.9 0.1 pad_maximum_fusion.1
  148.0 26.4 %all_to_all.27 = bf16[32,72,128]{2,1,0:T(8,128)(2,1)S(1)} all-to-all(bf16[32,72,128]{2,1,0:T(8,128)(2,1)S(1)} %pad_maximum_fusion.1), channel_id=1, replica_groups=mesh['y'=8,'xl'=2,'core'=2,'z'=8,'xh'=4] {'y','xl','core'}, dimensions={0} | all-to-all | bytes 1179648 | tf_op jit(solution)/shard_map/all_to_all | solution.py:19
  174.5 0.1 convert_reduce_fusion.1
  174.6 0.6 fusion.47
  (13 shorter events, 0.1 us)
Async XLA Ops:
  0.6 1.8 %copy-start = (bf16[512,1152]{1,0:T(8,128)(2,1)S(1)}, bf16[512,1152]{1,0:T(8,128)(2,1)}, u32[]{:S(2)}) copy-start(bf16[512,1152]{1,0:T(8,128)(2,1)} %param.5) | copy-start | bytes 3538948
  0.6 3.2 %copy-start.1 = (bf16[128,1152]{1,0:T(8,128)(2,1)S(1)}, bf16[128,1152]{1,0:T(8,128)(2,1)}, u32[]{:S(2)}) copy-start(bf16[128,1152]{1,0:T(8,128)(2,1)} %param.7) | copy-start | bytes 884740
  5.8 74.3 %all-to-all-start = ((bf16[32,24,1152]{2,1,0:T(8,128)(2,1)}), bf16[32,24,1152]{2,1,0:T(8,128)(2,1)S(1)}, u32[]{:S(2)}, u32[]{:S(2)}) async-start(bf16[32,24,1152]{2,1,0:T(8,128)(2,1)} %pad_maximum_fusion), calls=%async_computation | async-start | bytes 3538944 | tf_op jit(solution)/shard_map/all_to_all | solution.py:19
  81.2 10.5 %all-to-all-start.1 = ((bf16[4,16,1280]{2,1,0:T(8,128)(2,1)}), bf16[4,16,1280]{2,1,0:T(8,128)(2,1)S(1)}, u32[]{:S(2)}, u32[]{:S(2)}) async-start(bf16[4,16,1280]{2,1,0:T(8,128)(2,1)} %broadcast_in_dim.27), calls=%async_computation.1 | async-start | bytes 327680 | tf_op jit(solution)/shard_map/all_to_all | solution.py:19
  103.9 42.0 %copy-start.2 = (bf16[128,1152]{1,0:T(8,128)(2,1)S(1)}, bf16[128,1152]{1,0:T(8,128)(2,1)}, u32[]{:S(2)}) copy-start(bf16[128,1152]{1,0:T(8,128)(2,1)} %param.7) | copy-start | bytes 884740

commit v3 on v2

v3 whole, which is shorter than its diff:
```python
import jax
import jax.numpy as jnp
from jax import lax
from jax.sharding import Mesh
from jax.sharding import PartitionSpec as P

DP = ("y", "xl", "core")
BLK = ("z", "xh")
CHIPS = ("core", "z", "xh")

SCALE = 10.0
BIAS = -5.0
EPS = 1e-06
BF16 = jnp.bfloat16
F32 = jnp.float32


def exchange(x, axes, groups=None):
    return lax.all_to_all(x, axes, 0, 0, axis_index_groups=groups, tiled=True)


def to_all(x, n):
    return jnp.broadcast_to(x[None], (n, *x.shape))


def blk_groups(n_z, n_xh):
    zero = [[(z, xh) for z in range(n_z)] for xh in range(n_xh)]
    fine = n_z // n_xh
    one = [[(zh * fine + zl, xh) for zl in range(fine) for xh in range(n_xh)] for zh in range(n_xh)]
    grids = [[[core * n_z * n_xh + z * n_xh + xh for z, xh in row] for row in grid] for core, grid in enumerate((zero, one))]
    first = [list(column) for grid in grids for column in zip(*grid)]
    second = [row for grid in grids for row in grid]
    return first, second


def place(core, n_z, n_xh, z, xh):
    flat = z * n_xh + xh
    return jnp.where(core == 0, xh, flat // n_z), jnp.where(core == 0, z, flat % n_z)


def activate(values):
    return jax.nn.gelu(values, approximate=True)


def body(captions, w_in, w_out, images, pairs):
    rows, width = captions.shape
    n_z, n_xh, n_dp = lax.axis_size("z"), lax.axis_size("xh"), lax.axis_size(DP)
    n_core = lax.axis_size("core")
    core = lax.axis_index("core")
    first, second = blk_groups(n_z, n_xh)
    per_first = rows // n_xh
    own = per_first // n_z
    img_block = images.shape[0]
    img_part = img_block // n_core

    img = lax.dynamic_slice_in_dim(images, core * img_part, img_part, 0).astype(F32)
    img = (img * lax.rsqrt(jnp.sum(img * img, axis=1, keepdims=True) + EPS)).astype(BF16)

    pre_act = jnp.dot(captions, w_in, preferred_element_type=F32)
    hidden = activate(pre_act).astype(BF16)
    partial = jnp.dot(hidden, w_out, preferred_element_type=F32).astype(BF16)

    sent = jnp.concatenate([partial.reshape(n_xh, per_first, width), to_all(img, n_xh)], axis=1)
    got = exchange(sent, CHIPS, first)
    partial = jnp.sum(got[:, :per_first].astype(F32), axis=0).astype(BF16)
    img = got[:, per_first:].reshape(n_xh * img_part, width)
    sent = jnp.concatenate([partial.reshape(n_z, own, width), to_all(img, n_z)], axis=1)
    got = exchange(sent, CHIPS, second)
    img = got[:, own:].reshape(-1, width)
    other_img = lax.ppermute(img, "core", [(i, n_core - 1 - i) for i in range(n_core)])
    embedding = jnp.sum(got[:, :own].astype(F32), axis=0)

    inv_norm = lax.rsqrt(jnp.sum(embedding * embedding, axis=1, keepdims=True) + EPS)
    unit_dir = embedding * inv_norm
    unit_half = unit_dir.astype(BF16)

    at_first, at_second = place(core, n_z, n_xh, lax.axis_index("z"), lax.axis_index("xh"))
    pair = lax.dynamic_slice_in_dim(pairs, at_first * per_first + at_second * own, own, 0)[:, None]
    n = lax.broadcasted_iota(jnp.int32, (1, img.shape[0]), 1)
    slot, row = n // img_part, n % img_part

    def half_grad(img, core):
        block = jnp.where(core == 0, slot, (slot % n_xh) * n_z + slot // n_xh)
        logits = (
            SCALE * lax.dot_general(unit_half, img, (((1,), (1,)), ((), ())), preferred_element_type=F32) + BIAS
        )
        label = (pair == block * img_block + core * img_part + row).astype(F32)
        mismatch = (jax.nn.sigmoid(logits) - label).astype(BF16)
        return jnp.dot(mismatch, img, preferred_element_type=F32)

    unit_grad = SCALE * (half_grad(img, core) + half_grad(other_img, n_core - 1 - core))

    embed_half = (
        (unit_grad - unit_dir * jnp.sum(unit_dir * unit_grad, axis=1, keepdims=True)) * inv_norm
    ).astype(BF16)
    got = exchange(to_all(embed_half, n_z), CHIPS, second).reshape(per_first, width)
    embed_half = exchange(to_all(got, n_xh), CHIPS, first).reshape(rows, width)

    hidden_grad = lax.dot_general(embed_half, w_out, (((1,), (1,)), ((), ())), preferred_element_type=F32)
    _, pullback = jax.vjp(activate, pre_act)
    preact_grad = pullback(hidden_grad)[0].astype(BF16)
    grad_in = lax.dot_general(captions, preact_grad, (((0,), (0,)), ((), ())), preferred_element_type=F32)
    grad_out = lax.dot_general(embed_half, hidden, (((0,), (0,)), ((), ())), preferred_element_type=F32)
    share = width // n_dp
    sent = jnp.concatenate(
        [grad_in.astype(BF16).reshape(n_dp, share, -1), grad_out.astype(BF16).reshape(n_dp, share, -1)], axis=1
    )
    total = jnp.sum(exchange(sent, DP).astype(F32), axis=0)
    return total[:share], total[share:]


def solution(mesh):
    fine = Mesh(mesh.devices.reshape(8, 2, 2, 8, 4), (*DP, *BLK))
    placed = (P(DP, None), P(None, BLK), P(BLK, None), P(BLK, None), P(DP))
    return jax.shard_map(
        body, mesh=fine, in_specs=placed, out_specs=(P(DP, BLK), P(DP, BLK)), check_vma=False
    )
```

time: 176 us -> 158 us (0.90)
  waiting for transfers between devices: 54.8 us -> 0.01 us
  blocking collectives: 78.8 us -> 131 us
  starting transfers between devices: 29.2 us -> 9.62 us
  matrix products: 4.88 us -> 7.48 us
  local copies, waits for them, and re-layouts: 1.76 us -> 4.34 us
    all_to_all x2 -> x0, waiting for transfers between devices: 54.8 us -> none  [exchange(): return lax.all_to_all(x, axes, 0, 0, tiled=True)]
    all_to_all x3 -> x5, blocking collectives: 78.8 us -> 131 us  [exchange(): return lax.all_to_all(x, axes, 0, 0, axis_index_groups=groups, tiled=True)]
    all_to_all x2 -> x0, starting transfers between devices: 29.2 us -> none  [exchange(): return lax.all_to_all(x, axes, 0, 0, tiled=True)]
    ppermute x0 -> x1, starting transfers between devices: none -> 9.62 us  [body(): lax.ppermute(img, 'core', [(i, n_core - 1 - i) for i in range(n_core)])]
    dot_general x1 -> x2, matrix products: 1.36 us -> 3.96 us  [half_grad(): return jnp.dot(mismatch, img, preferred_element_type=F32)]
    unnamed x6 -> x16, local copies, waits for them, and re-layouts: 0.02 us -> 2.21 us
  transfers between devices with their start and end apart: 2 -> 1, of which waited for: 2 -> 0; matrix products, arithmetic and copies ran while one was open for 0% -> 3% of each run, Pallas kernels for 0% -> 0%
where the time goes in v3:
time: 158 us; the launch traced here: 157 us
  blocking collectives  131 us (83%)
  starting transfers between devices  9.62 us (6%)
  matrix products  7.48 us (5%)
  local copies, waits for them, and re-layouts  4.34 us (3%)
  other arithmetic  3.72 us (2%)
    all_to_all x5, blocking collectives, exchange(): return lax.all_to_all(x, axes, 0, 0, axis_index_groups=groups, tiled=True)  131 us
    ppermute x1, starting transfers between devices, body(): lax.ppermute(img, 'core', [(i, n_core - 1 - i) for i in range(n_core)])  9.62 us
    dot_general x2, matrix products, half_grad(): return jnp.dot(mismatch, img, preferred_element_type=F32)  3.96 us
  transfers between devices with their start and end apart: 1, of which 0 were waited for; matrix products, arithmetic and copies ran while one was open for 3% of the time, Pallas kernels for 0%

profile of v3, /device:TPU:1, one launch (start us, length us, event | category | flops | bytes accessed | tf_op | source)
XLA Modules:
  0.0 157.1 jit_solution(15409827230292273847)
XLA Ops:
  0.7 1.0 fusion.31
  1.7 0.9 fusion.32
  2.5 1.4 fusion.84
  4.0 0.5 convolution_convert_fusion
  4.5 0.2 copy-done.4
  4.7 0.1 pad_maximum_fusion.1
  4.8 36.8 %all_to_all.25 = bf16[4,144,1152]{2,1,0:T(8,128)(2,1)S(1)} all-to-all(bf16[4,144,1152]{2,1,0:T(8,128)(2,1)S(1)} %pad_maximum_fusion.1), channel_id=1, replica_groups={{0,1,2,3},{4,5,6,7},{8,9,10,11},{12,13,14,15},{16,17,18,19},{20,21,22,2..., dimensions={0} | all-to-all | bytes 2654208 | tf_op jit(solution)/shard_map/all_to_all | solution.py:19
  41.6 0.2 slice_reduce_fusion
  41.8 0.1 broadcast_in_dim.14
  41.9 0.1 pad_maximum_fusion
  42.0 28.3 %all_to_all.26 = bf16[8,80,1152]{2,1,0:T(8,128)(2,1)S(1)} all-to-all(bf16[8,80,1152]{2,1,0:T(8,128)(2,1)S(1)} %pad_maximum_fusion), channel_id=1, replica_groups={{0,4,8,12,16,20,24,28},{1,5,9,13,17,21,25,29},{2,6,10,14,18,22,26,30},{..., dimensions={0} | all-to-all | bytes 2949120 | tf_op jit(solution)/shard_map/all_to_all | solution.py:19
  70.3 0.1 slice.27
  70.5 1.0 copy-done.1
  71.5 9.6 %collective-permute-start = (bf16[512,1152]{1,0:T(8,128)(2,1)S(1)}, bf16[512,1152]{1,0:T(8,128)(2,1)S(1)}, u32[]{:S(2)}, u32[]{:S(2)}) collective-permute-start(bf16[512,1152]{1,0:T(8,128)(2,1)S(1)} %bitcast.19), channel_id=1, source_target_pairs={{0,32},{32,0},{1,33},{33,1},{2,34},{34,2},{3,35},{35,3},{4,36},{36... | collective-permute-start | bytes 3538952 | tf_op jit(solution)/shard_map/ppermute | solution.py:70
  81.1 0.8 dynamic_slice.7
  81.9 1.0 convert_reduce_fusion.1
  82.9 0.6 copy-done.2
  83.6 0.1 multiply_reduce_fusion.1
  83.7 2.2 %fusion.16 = f32[16,1152]{1,0:T(8,128)} fusion(bf16[512,1152]{1,0:T(8,128)(2,1)S(1)} %bitcast.20, s32[512]{0:T(512)S(1)} %fusion.64, s32[16]{0:T(128)S(1)} %dynamic_slice.7, f32[16,1152]{1,0:T(8,128)} %copy-done.2, f32[16]{0:T(128)S(1)} %add_rsqrt_fusion), kind=kOutput, calls=%fused_computation.26 | convolution fusion | flops 37859328 | bytes 1329280 | tf_op jit(solution)/shard_map/dot_general | solution.py:89
  85.9 1.8 %multiply_reduce_fusion = (f32[16]{0:T(128)S(1)}, f32[16,1152]{1,0:T(8,128)S(1)}) fusion(f32[16,1152]{1,0:T(8,128)} %copy-done.2, f32[16]{0:T(128)S(1)} %add_rsqrt_fusion, f32[16,1152]{1,0:T(8,128)} %fusion.16, bf16[512,1152]{1,0:T(8,128)(2,1)S(1)} %collective-permute-done, s32[512]{0:T(512)S(1)} %fusion.60, s32[16]{0:T(128)S(1)} %dynamic_slice.7), kind=kOutput, calls=%fused_computation.50 | convolution fusion | flops 37951472 | bytes 1403072 | tf_op jit(solution)/shard_map/dot_general | solution.py:89
  87.7 0.1 multiply_convert_fusion.1
  87.8 13.7 %all_to_all.27 = bf16[8,16,1152]{2,1,0:T(8,128)(2,1)S(1)} all-to-all(bf16[8,16,1152]{2,1,0:T(8,128)(2,1)S(1)} %broadcast_in_dim.15), channel_id=1, replica_groups={{0,4,8,12,16,20,24,28},{1,5,9,13,17,21,25,29},{2,6,10,14,18,22,26,30},{..., dimensions={0} | all-to-all | bytes 589824 | tf_op jit(solution)/shard_map/all_to_all | solution.py:19
  101.5 0.1 broadcast_in_dim.17
  101.6 22.3 %all_to_all.28 = bf16[4,128,1152]{2,1,0:T(8,128)(2,1)S(1)} all-to-all(bf16[4,128,1152]{2,1,0:T(8,128)(2,1)S(1)} %broadcast_in_dim.17), channel_id=1, replica_groups={{0,1,2,3},{4,5,6,7},{8,9,10,11},{12,13,14,15},{16,17,18,19},{20,21,22,2..., dimensions={0} | all-to-all | bytes 2359296 | tf_op jit(solution)/shard_map/all_to_all | solution.py:19
  123.9 0.6 convolution_convert_fusion.1
  124.5 0.4 copy-done.7
  124.9 1.1 fusion
  126.0 0.2 copy.9
  126.3 0.1 pad_maximum_fusion.2
  126.4 29.9 %all_to_all.29 = bf16[32,72,128]{2,1,0:T(8,128)(2,1)S(1)} all-to-all(bf16[32,72,128]{2,1,0:T(8,128)(2,1)S(1)} %pad_maximum_fusion.2), channel_id=1, replica_groups=mesh['y'=8,'xl'=2,'core'=2,'z'=8,'xh'=4] {'y','xl','core'}, dimensions={0} | all-to-all | bytes 1179648 | tf_op jit(solution)/shard_map/all_to_all | solution.py:19
  156.3 0.1 convert_reduce_fusion
  156.4 0.6 fusion.81
  (22 shorter events, 0.2 us)
Async XLA Ops:
  0.6 1.9 %copy-start = (bf16[512,1152]{1,0:T(8,128)(2,1)S(1)}, bf16[512,1152]{1,0:T(8,128)(2,1)}, u32[]{:S(2)}) copy-start(bf16[512,1152]{1,0:T(8,128)(2,1)} %param.5) | copy-start | bytes 3538948
  0.6 3.3 %copy-start.6 = (bf16[128,1152]{1,0:T(8,128)(2,1)S(1)}, bf16[128,1152]{1,0:T(8,128)(2,1)}, u32[]{:S(2)}) copy-start(bf16[128,1152]{1,0:T(8,128)(2,1)} %param.7) | copy-start | bytes 884740
  4.0 0.7 copy-start.4
  70.3 1.1 copy-start.1
  71.5 14.4 %collective-permute-start = (bf16[512,1152]{1,0:T(8,128)(2,1)S(1)}, bf16[512,1152]{1,0:T(8,128)(2,1)S(1)}, u32[]{:S(2)}, u32[]{:S(2)}) collective-permute-start(bf16[512,1152]{1,0:T(8,128)(2,1)S(1)} %bitcast.19), channel_id=1, source_target_pairs={{0,32},{32,0},{1,33},{33,1},{2,34},{34,2},{3,35},{35,3},{4,36},{36... | collective-permute-start | bytes 3538952 | tf_op jit(solution)/shard_map/ppermute | solution.py:70
  82.9 0.6 copy-start.2
  85.9 1.8 %copy-start.3 = (f32[16,1152]{1,0:T(8,128)S(1)}, f32[16,1152]{1,0:T(8,128)}, u32[]{:S(2)}) copy-start(f32[16,1152]{1,0:T(8,128)} %copy-done.2) | copy-start | bytes 221188
  101.6 22.3 %copy-start.5 = (f32[512,128]{1,0:T(8,128)S(1)}, f32[512,128]{1,0:T(8,128)}, u32[]{:S(2)}) copy-start(f32[512,128]{1,0:T(8,128)} %copy-done.4) | copy-start | bytes 786436
  123.9 1.0 copy-start.7

commit v4 on v3

--- a/solution.py
+++ b/solution.py
@@ -1,6 +1,10 @@
+import functools
+
 import jax
 import jax.numpy as jnp
 from jax import lax
+from jax.experimental import pallas as pl
+from jax.experimental.pallas import tpu as pltpu
 from jax.sharding import Mesh
 from jax.sharding import PartitionSpec as P
 
@@ -42,6 +46,50 @@
     return jax.nn.gelu(values, approximate=True)
 
 
+def half_grad(core, geometry, unit_half, pair, img):
+    n_z, n_xh, img_block, img_part = geometry
+    n = lax.broadcasted_iota(jnp.int32, (1, img.shape[0]), 1)
+    slot, row = n // img_part, n % img_part
+    block = jnp.where(core == 0, slot, (slot % n_xh) * n_z + slot // n_xh)
+    logits = SCALE * lax.dot_general(unit_half, img, (((1,), (1,)), ((), ())), preferred_element_type=F32) + BIAS
+    label = (pair == block * img_block + core * img_part + row).astype(F32)
+    mismatch = (jax.nn.sigmoid(logits) - label).astype(BF16)
+    return jnp.dot(mismatch, img, preferred_element_type=F32)
+
+
+def own_kernel(geometry, core_ref, part_ref, pair_ref, img_ref, dir_ref, norm_ref, grad_ref):
+    embedding = part_ref[0].astype(F32)
+    for k in range(1, part_ref.shape[0]):
+        embedding += part_ref[k].astype(F32)
+    inv_norm = lax.rsqrt(jnp.sum(embedding * embedding, axis=1, keepdims=True) + EPS)
+    unit_dir = embedding * inv_norm
+    dir_ref[...] = unit_dir
+    norm_ref[...] = jnp.broadcast_to(inv_norm, norm_ref.shape)
+    grad_ref[...] = half_grad(core_ref[0], geometry, unit_dir.astype(BF16), pair_ref[:, :1], img_ref[...])
+
+
+def other_kernel(geometry, core_ref, dir_ref, norm_ref, grad_ref, pair_ref, img_ref, out_ref):
+    unit_dir = dir_ref[...]
+    more = half_grad(1 - core_ref[0], geometry, unit_dir.astype(BF16), pair_ref[:, :1], img_ref[...])
+    unit_grad = SCALE * (grad_ref[...] + more)
+    along = jnp.sum(unit_dir * unit_grad, axis=1, keepdims=True)
+    embed_half = ((unit_grad - unit_dir * along) * norm_ref[:, :1]).astype(BF16)
+    for k in range(out_ref.shape[0]):
+        out_ref[k] = embed_half
+
+
+def call(kernel, outs, flops, *args):
+    whole = pl.BlockSpec(memory_space=pltpu.VMEM)
+    return pl.pallas_call(
+        kernel,
+        out_shape=outs,
+        in_specs=[pl.BlockSpec(memory_space=pltpu.SMEM)] + [whole] * (len(args) - 1),
+        out_specs=jax.tree.map(lambda _: whole, outs),
+        compiler_params=pltpu.CompilerParams(vmem_limit_bytes=16 * 1024 * 1024),
+        cost_estimate=pl.CostEstimate(flops=flops, bytes_accessed=3_000_000, transcendentals=0),
+    )(*args)
+
+
 def body(captions, w_in, w_out, images, pairs):
     rows, width = captions.shape
     n_z, n_xh, n_dp = lax.axis_size("z"), lax.axis_size("xh"), lax.axis_size(DP)
@@ -53,8 +101,7 @@
     img_block = images.shape[0]
     img_part = img_block // n_core
 
-    img = lax.dynamic_slice_in_dim(images, core * img_part, img_part, 0).astype(F32)
-    img = (img * lax.rsqrt(jnp.sum(img * img, axis=1, keepdims=True) + EPS)).astype(BF16)
+    img = lax.dynamic_slice_in_dim(images, core * img_part, img_part, 0)
 
     pre_act = jnp.dot(captions, w_in, preferred_element_type=F32)
     hidden = activate(pre_act).astype(BF16)
@@ -63,37 +110,42 @@
     sent = jnp.concatenate([partial.reshape(n_xh, per_first, width), to_all(img, n_xh)], axis=1)
     got = exchange(sent, CHIPS, first)
     partial = jnp.sum(got[:, :per_first].astype(F32), axis=0).astype(BF16)
-    img = got[:, per_first:].reshape(n_xh * img_part, width)
+    img = got[:, per_first:].reshape(n_xh * img_part, width).astype(F32)
+    img = (img * lax.rsqrt(jnp.sum(img * img, axis=1, keepdims=True) + EPS)).astype(BF16)
     sent = jnp.concatenate([partial.reshape(n_z, own, width), to_all(img, n_z)], axis=1)
     got = exchange(sent, CHIPS, second)
-    img = got[:, own:].reshape(-1, width)
+    partial, img = lax.optimization_barrier((got[:, :own], got[:, own:]))
+    img = img.reshape(-1, width)
     other_img = lax.ppermute(img, "core", [(i, n_core - 1 - i) for i in range(n_core)])
-    embedding = jnp.sum(got[:, :own].astype(F32), axis=0)
-
-    inv_norm = lax.rsqrt(jnp.sum(embedding * embedding, axis=1, keepdims=True) + EPS)
-    unit_dir = embedding * inv_norm
-    unit_half = unit_dir.astype(BF16)
 
     at_first, at_second = place(core, n_z, n_xh, lax.axis_index("z"), lax.axis_index("xh"))
-    pair = lax.dynamic_slice_in_dim(pairs, at_first * per_first + at_second * own, own, 0)[:, None]
-    n = lax.broadcasted_iota(jnp.int32, (1, img.shape[0]), 1)
-    slot, row = n // img_part, n % img_part
-
-    def half_grad(img, core):
-        block = jnp.where(core == 0, slot, (slot % n_xh) * n_z + slot // n_xh)
-        logits = (
-            SCALE * lax.dot_general(unit_half, img, (((1,), (1,)), ((), ())), preferred_element_type=F32) + BIAS
-        )
-        label = (pair == block * img_block + core * img_part + row).astype(F32)
-        mismatch = (jax.nn.sigmoid(logits) - label).astype(BF16)
-        return jnp.dot(mismatch, img, preferred_element_type=F32)
-
-    unit_grad = SCALE * (half_grad(img, core) + half_grad(other_img, n_core - 1 - core))
-
-    embed_half = (
-        (unit_grad - unit_dir * jnp.sum(unit_dir * unit_grad, axis=1, keepdims=True)) * inv_norm
-    ).astype(BF16)
-    got = exchange(to_all(embed_half, n_z), CHIPS, second).reshape(per_first, width)
+    pair = lax.dynamic_slice_in_dim(pairs, at_first * per_first + at_second * own, own, 0)
+    pair = jnp.broadcast_to(pair[:, None], (own, 128))
+    geometry = (n_z, n_xh, img_block, img_part)
+    here = core.reshape(1).astype(jnp.int32)
+    flops = 4 * own * img.shape[0] * width
+    row = jax.ShapeDtypeStruct((own, width), F32)
+    unit_dir, inv_norm, grad = call(
+        functools.partial(own_kernel, geometry),
+        (row, jax.ShapeDtypeStruct((own, 128), F32), row),
+        flops,
+        here,
+        partial,
+        pair,
+        img,
+    )
+    sent = call(
+        functools.partial(other_kernel, geometry),
+        jax.ShapeDtypeStruct((n_z, own, width), BF16),
+        flops,
+        here,
+        unit_dir,
+        inv_norm,
+        grad,
+        pair,
+        other_img,
+    )
+    got = exchange(sent, CHIPS, second).reshape(per_first, width)
     embed_half = exchange(to_all(got, n_xh), CHIPS, first).reshape(rows, width)
 
     hidden_grad = lax.dot_general(embed_half, w_out, (((1,), (1,)), ((), ())), preferred_element_type=F32)

time: 158 us -> 153 us (0.968)
  matrix products: 7.48 us -> 3.52 us
  other arithmetic: 3.72 us -> 0.84 us
    dot_general x2 -> x0, matrix products: 3.96 us -> none  [half_grad(): return jnp.dot(mismatch, img, preferred_element_type=F32)]
  transfers between devices with their start and end apart: 1 -> 1, of which waited for: 0 -> 0; matrix products, arithmetic and copies ran while one was open for 3% -> 1% of each run, Pallas kernels for 0% -> 0%
where the time goes in v4:
time: 153 us
  blocking collectives  131 us (86%)
  starting transfers between devices  9.62 us (6%)
  local copies, waits for them, and re-layouts  5.43 us (4%)
  matrix products  3.52 us (2%)
    all_to_all x5, blocking collectives, exchange(): return lax.all_to_all(x, axes, 0, 0, axis_index_groups=groups, tiled=True)  131 us
    ppermute x1, starting transfers between devices, body(): lax.ppermute(img, 'core', [(i, n_core - 1 - i) for i in range(n_core)])  9.62 us
  transfers between devices with their start and end apart: 1, of which 0 were waited for; matrix products, arithmetic and copies ran while one was open for 1% of the time, Pallas kernels for 0%

profile of v4, /device:TPU:1, one launch (start us, length us, event | category | flops | bytes accessed | tf_op | source)
XLA Modules:
  0.0 152.7 jit_solution(702089066131499156)
XLA Ops:
  0.7 0.9 constant_dynamic-slice_fusion
  1.5 0.4 copy-done
  1.9 1.4 fusion.25
  3.4 0.5 convolution_convert_fusion
  3.9 0.2 copy-done.2
  4.1 0.1 pad_maximum_fusion.1
  4.2 36.8 %all_to_all.25 = bf16[4,144,1152]{2,1,0:T(8,128)(2,1)S(1)} all-to-all(bf16[4,144,1152]{2,1,0:T(8,128)(2,1)S(1)} %pad_maximum_fusion.1), channel_id=1, replica_groups={{0,1,2,3},{4,5,6,7},{8,9,10,11},{12,13,14,15},{16,17,18,19},{20,21,22,2..., dimensions={0} | all-to-all | bytes 2654208 | tf_op jit(solution)/shard_map/all_to_all | solution.py:23
  41.0 0.1 multiply_reduce_fusion
  41.1 0.1 rsqrt.12
  41.2 0.1 fusion.1
  41.3 0.2 slice_reduce_fusion
  41.5 0.1 broadcast_in_dim.11
  41.6 0.1 pad_maximum_fusion
  41.8 28.3 %all_to_all.26 = bf16[8,80,1152]{2,1,0:T(8,128)(2,1)S(1)} all-to-all(bf16[8,80,1152]{2,1,0:T(8,128)(2,1)S(1)} %pad_maximum_fusion), channel_id=1, replica_groups={{0,4,8,12,16,20,24,28},{1,5,9,13,17,21,25,29},{2,6,10,14,18,22,26,30},{..., dimensions={0} | all-to-all | bytes 2949120 | tf_op jit(solution)/shard_map/all_to_all | solution.py:23
  70.0 0.1 slice.27
  70.2 0.7 slice.26.part_ref
  70.9 9.6 %collective-permute-start = (bf16[512,1152]{1,0:T(8,128)(2,1)S(1)}, bf16[512,1152]{1,0:T(8,128)(2,1)S(1)}, u32[]{:S(2)}, u32[]{:S(2)}) collective-permute-start(bf16[512,1152]{1,0:T(8,128)(2,1)S(1)} %bitcast.19), channel_id=1, source_target_pairs={{0,32},{32,0},{1,33},{33,1},{2,34},{34,2},{3,35},{35,3},{4,36},{36... | collective-permute-start | bytes 3538952 | tf_op jit(solution)/shard_map/ppermute | solution.py:119
  80.6 0.8 dynamic_slice.7
  81.4 0.1 broadcast_in_dim.12.pair_ref
  81.4 1.0 copy-done.1
  82.4 0.7 shard_map.68
  83.1 0.8 shard_map.69
  83.9 13.7 %all_to_all.27 = bf16[8,16,1152]{2,1,0:T(8,128)(2,1)S(1)} all-to-all(bf16[8,16,1152]{2,1,0:T(8,128)(2,1)S(1)} %shard_map.69), channel_id=1, replica_groups={{0,4,8,12,16,20,24,28},{1,5,9,13,17,21,25,29},{2,6,10,14,18,22,26,30},{..., dimensions={0} | all-to-all | bytes 589824 | tf_op jit(solution)/shard_map/all_to_all | solution.py:23
  97.6 0.1 broadcast_in_dim.14
  97.7 22.6 %all_to_all.28 = bf16[4,128,1152]{2,1,0:T(8,128)(2,1)S(1)} all-to-all(bf16[4,128,1152]{2,1,0:T(8,128)(2,1)S(1)} %broadcast_in_dim.14), channel_id=1, replica_groups={{0,1,2,3},{4,5,6,7},{8,9,10,11},{12,13,14,15},{16,17,18,19},{20,21,22,2..., dimensions={0} | all-to-all | bytes 2359296 | tf_op jit(solution)/shard_map/all_to_all | solution.py:23
  120.3 1.1 fusion
  121.4 0.6 convolution_convert_fusion.1
  121.9 0.2 copy.8
  122.3 0.1 pad_maximum_fusion.2
  122.4 29.6 %all_to_all.29 = bf16[32,72,128]{2,1,0:T(8,128)(2,1)S(1)} all-to-all(bf16[32,72,128]{2,1,0:T(8,128)(2,1)S(1)} %pad_maximum_fusion.2), channel_id=1, replica_groups=mesh['y'=8,'xl'=2,'core'=2,'z'=8,'xh'=4] {'y','xl','core'}, dimensions={0} | all-to-all | bytes 1179648 | tf_op jit(solution)/shard_map/all_to_all | solution.py:23
  152.0 0.1 convert_reduce_fusion
  152.1 0.6 fusion.22
  (15 shorter events, 0.2 us)
Async XLA Ops:
  0.6 1.3 copy-start
  0.6 2.7 %copy-start.4 = (bf16[128,1152]{1,0:T(8,128)(2,1)S(1)}, bf16[128,1152]{1,0:T(8,128)(2,1)}, u32[]{:S(2)}) copy-start(bf16[128,1152]{1,0:T(8,128)(2,1)} %param.7) | copy-start | bytes 884740
  3.4 0.7 copy-start.2
  70.9 12.2 %collective-permute-start = (bf16[512,1152]{1,0:T(8,128)(2,1)S(1)}, bf16[512,1152]{1,0:T(8,128)(2,1)S(1)}, u32[]{:S(2)}, u32[]{:S(2)}) collective-permute-start(bf16[512,1152]{1,0:T(8,128)(2,1)S(1)} %bitcast.19), channel_id=1, source_target_pairs={{0,32},{32,0},{1,33},{33,1},{2,34},{34,2},{3,35},{35,3},{4,36},{36... | collective-permute-start | bytes 3538952 | tf_op jit(solution)/shard_map/ppermute | solution.py:119
  81.4 1.0 copy-start.1
  97.7 22.6 %copy-start.3 = (f32[512,128]{1,0:T(8,128)S(1)}, f32[512,128]{1,0:T(8,128)}, u32[]{:S(2)}) copy-start(f32[512,128]{1,0:T(8,128)} %copy-done.2) | copy-start | bytes 786436
  97.7 22.6 %copy-start.5 = (bf16[128,1152]{1,0:T(8,128)(2,1)S(1)}, bf16[128,1152]{1,0:T(8,128)(2,1)}, u32[]{:S(2)}) copy-start(bf16[128,1152]{1,0:T(8,128)(2,1)} %param.7) | copy-start | bytes 884740

commit v5 on v4

--- a/solution.py
+++ b/solution.py
@@ -1,4 +1,5 @@
 import functools
+import math
 
 import jax
 import jax.numpy as jnp
@@ -15,6 +16,9 @@
 SCALE = 10.0
 BIAS = -5.0
 EPS = 1e-06
+CURVE = math.sqrt(2.0 / math.pi)
+CUBIC = 0.044715
+GRANT = 60 * 1024 * 1024
 BF16 = jnp.bfloat16
 F32 = jnp.float32
 
@@ -37,13 +41,68 @@
     return first, second
 
 
+def bend(v):
+    return jnp.tanh(CURVE * (v + CUBIC * (v * v * v)))
+
+
 def place(core, n_z, n_xh, z, xh):
     flat = z * n_xh + xh
     return jnp.where(core == 0, xh, flat // n_z), jnp.where(core == 0, z, flat % n_z)
 
 
-def activate(values):
-    return jax.nn.gelu(values, approximate=True)
+def forward_kernel(
+    per_first, img_part, core_ref, captions_hbm, w_in_hbm, w_out_hbm, images_hbm, out_hbm, pre_hbm,
+    captions_ref, w_in_ref, w_out_ref, img_ref, out_ref, pre_ref, sems
+):
+    n = out_ref.shape[0]
+    start = pl.multiple_of(core_ref[0] * img_part, img_part)
+    blocks = [pl.ds(k * per_first, per_first) for k in range(n)]
+    fetch_in = pltpu.make_async_copy(w_in_hbm, w_in_ref, sems.at[0])
+    fetch_out = pltpu.make_async_copy(w_out_hbm, w_out_ref, sems.at[1])
+    fetch_img = pltpu.make_async_copy(images_hbm.at[pl.ds(start, img_part)], img_ref, sems.at[2])
+    fetches = [
+        pltpu.make_async_copy(captions_hbm.at[at], captions_ref.at[at], sems.at[3 + k]) for k, at in enumerate(blocks)
+    ]
+    for copy in (fetch_in, fetches[0], fetch_out, fetch_img, *fetches[1:]):
+        copy.start()
+    stores = []
+    fetch_in.wait()
+    for k, at in enumerate(blocks):
+        fetches[k].wait()
+        pre_act = jnp.dot(captions_ref[at, :], w_in_ref[...], preferred_element_type=F32)
+        pre_ref[at, :] = pre_act
+        hidden = (0.5 * pre_act * (1.0 + bend(pre_act))).astype(BF16)
+        if k == 0:
+            fetch_out.wait()
+            fetch_img.wait()
+        out_ref[k, :per_first] = jnp.dot(hidden, w_out_ref[...], preferred_element_type=F32).astype(BF16)
+        out_ref[k, per_first:] = img_ref[...]
+        stores.append(pltpu.make_async_copy(out_ref.at[k], out_hbm.at[k], sems.at[3 + n + k]))
+        stores.append(pltpu.make_async_copy(pre_ref.at[at], pre_hbm.at[at], sems.at[3 + 2 * n + k]))
+        stores[-2].start()
+        stores[-1].start()
+    for copy in stores:
+        copy.wait()
+
+
+def backward_kernel(share, core_ref, captions_ref, embed_ref, w_out_ref, pre_ref, mine_ref, other_ref):
+    embed_half = embed_ref[...]
+    hidden_grad = lax.dot_general(embed_half, w_out_ref[...], (((1,), (1,)), ((), ())), preferred_element_type=F32)
+    v = pre_ref[...]
+    t = bend(v)
+    hidden = (0.5 * v * (1.0 + t)).astype(BF16)
+    slope = 0.5 * (1.0 + t) + 0.5 * v * (1.0 - t * t) * (CURVE * (1.0 + 3.0 * CUBIC * v * v))
+    preact_grad = (hidden_grad * slope).astype(BF16)
+    over_rows = (((0,), (0,)), ((), ()))
+    grad_in = lax.dot_general(preact_grad, captions_ref[...], over_rows, preferred_element_type=F32).T
+    grad_out = lax.dot_general(hidden, embed_half, over_rows, preferred_element_type=F32).T
+    zero = core_ref[0] == 0
+    for at, grad in ((0, grad_in), (share, grad_out)):
+        for q in range(mine_ref.shape[0]):
+            even = grad[2 * q * share : (2 * q + 1) * share]
+            odd = grad[(2 * q + 1) * share : (2 * q + 2) * share]
+            mine_ref[q, at : at + share] = jnp.where(zero, even, odd)
+            other_ref[q, at : at + share] = jnp.where(zero, odd, even)
 
 
 def half_grad(core, geometry, unit_half, pair, img):
@@ -57,10 +116,8 @@
     return jnp.dot(mismatch, img, preferred_element_type=F32)
 
 
-def own_kernel(geometry, core_ref, part_ref, pair_ref, img_ref, dir_ref, norm_ref, grad_ref):
-    embedding = part_ref[0].astype(F32)
-    for k in range(1, part_ref.shape[0]):
-        embedding += part_ref[k].astype(F32)
+def own_kernel(geometry, core_ref, sum_ref, pair_ref, img_ref, dir_ref, norm_ref, grad_ref):
+    embedding = sum_ref[...]
     inv_norm = lax.rsqrt(jnp.sum(embedding * embedding, axis=1, keepdims=True) + EPS)
     unit_dir = embedding * inv_norm
     dir_ref[...] = unit_dir
@@ -78,14 +135,15 @@
         out_ref[k] = embed_half
 
 
-def call(kernel, outs, flops, *args):
-    whole = pl.BlockSpec(memory_space=pltpu.VMEM)
+def call(kernel, outs, flops, *args, place=pltpu.VMEM, scratch=(), grant=16 * 1024 * 1024):
+    whole = pl.BlockSpec(memory_space=place)
     return pl.pallas_call(
         kernel,
         out_shape=outs,
         in_specs=[pl.BlockSpec(memory_space=pltpu.SMEM)] + [whole] * (len(args) - 1),
         out_specs=jax.tree.map(lambda _: whole, outs),
-        compiler_params=pltpu.CompilerParams(vmem_limit_bytes=16 * 1024 * 1024),
+        scratch_shapes=scratch,
+        compiler_params=pltpu.CompilerParams(vmem_limit_bytes=grant),
         cost_estimate=pl.CostEstimate(flops=flops, bytes_accessed=3_000_000, transcendentals=0),
     )(*args)
 
@@ -95,34 +153,51 @@
     n_z, n_xh, n_dp = lax.axis_size("z"), lax.axis_size("xh"), lax.axis_size(DP)
     n_core = lax.axis_size("core")
     core = lax.axis_index("core")
+    swap = [(i, n_core - 1 - i) for i in range(n_core)]
     first, second = blk_groups(n_z, n_xh)
     per_first = rows // n_xh
     own = per_first // n_z
     img_block = images.shape[0]
     img_part = img_block // n_core
 
-    img = lax.dynamic_slice_in_dim(images, core * img_part, img_part, 0)
-
-    pre_act = jnp.dot(captions, w_in, preferred_element_type=F32)
-    hidden = activate(pre_act).astype(BF16)
-    partial = jnp.dot(hidden, w_out, preferred_element_type=F32).astype(BF16)
-
-    sent = jnp.concatenate([partial.reshape(n_xh, per_first, width), to_all(img, n_xh)], axis=1)
+    here = core.reshape(1).astype(jnp.int32)
+    sums = jax.ShapeDtypeStruct((n_xh, per_first + img_part, width), BF16)
+    acts = jax.ShapeDtypeStruct((rows, w_in.shape[1]), F32)
+    sent, pre_act = call(
+        functools.partial(forward_kernel, per_first, img_part),
+        (sums, acts),
+        4 * rows * width * w_in.shape[1],
+        here,
+        captions,
+        w_in,
+        w_out,
+        images,
+        place=pltpu.HBM,
+        grant=GRANT,
+        scratch=[
+            pltpu.VMEM(captions.shape, BF16),
+            pltpu.VMEM(w_in.shape, BF16),
+            pltpu.VMEM(w_out.shape, BF16),
+            pltpu.VMEM((img_part, width), BF16),
+            pltpu.VMEM(sums.shape, BF16),
+            pltpu.VMEM(acts.shape, F32),
+            pltpu.SemaphoreType.DMA((3 + 3 * n_xh,)),
+        ],
+    )
     got = exchange(sent, CHIPS, first)
     partial = jnp.sum(got[:, :per_first].astype(F32), axis=0).astype(BF16)
     img = got[:, per_first:].reshape(n_xh * img_part, width).astype(F32)
     img = (img * lax.rsqrt(jnp.sum(img * img, axis=1, keepdims=True) + EPS)).astype(BF16)
     sent = jnp.concatenate([partial.reshape(n_z, own, width), to_all(img, n_z)], axis=1)
     got = exchange(sent, CHIPS, second)
-    partial, img = lax.optimization_barrier((got[:, :own], got[:, own:]))
-    img = img.reshape(-1, width)
-    other_img = lax.ppermute(img, "core", [(i, n_core - 1 - i) for i in range(n_core)])
+    embedding = jnp.sum(got[:, :own].astype(F32), axis=0)
+    embedding, img = lax.optimization_barrier((embedding, got[:, own:].reshape(-1, width)))
+    other_img = lax.ppermute(img, "core", swap)
 
     at_first, at_second = place(core, n_z, n_xh, lax.axis_index("z"), lax.axis_index("xh"))
     pair = lax.dynamic_slice_in_dim(pairs, at_first * per_first + at_second * own, own, 0)
     pair = jnp.broadcast_to(pair[:, None], (own, 128))
     geometry = (n_z, n_xh, img_block, img_part)
-    here = core.reshape(1).astype(jnp.int32)
     flops = 4 * own * img.shape[0] * width
     row = jax.ShapeDtypeStruct((own, width), F32)
     unit_dir, inv_norm, grad = call(
@@ -130,7 +205,7 @@
         (row, jax.ShapeDtypeStruct((own, 128), F32), row),
         flops,
         here,
-        partial,
+        embedding,
         pair,
         img,
     )
@@ -148,16 +223,20 @@
     got = exchange(sent, CHIPS, second).reshape(per_first, width)
     embed_half = exchange(to_all(got, n_xh), CHIPS, first).reshape(rows, width)
 
-    hidden_grad = lax.dot_general(embed_half, w_out, (((1,), (1,)), ((), ())), preferred_element_type=F32)
-    _, pullback = jax.vjp(activate, pre_act)
-    preact_grad = pullback(hidden_grad)[0].astype(BF16)
-    grad_in = lax.dot_general(captions, preact_grad, (((0,), (0,)), ((), ())), preferred_element_type=F32)
-    grad_out = lax.dot_general(embed_half, hidden, (((0,), (0,)), ((), ())), preferred_element_type=F32)
     share = width // n_dp
-    sent = jnp.concatenate(
-        [grad_in.astype(BF16).reshape(n_dp, share, -1), grad_out.astype(BF16).reshape(n_dp, share, -1)], axis=1
-    )
-    total = jnp.sum(exchange(sent, DP).astype(F32), axis=0)
+    grads = jax.ShapeDtypeStruct((n_dp // n_core, 2 * share, w_in.shape[1]), F32)
+    mine, other = call(
+        functools.partial(backward_kernel, share),
+        (grads, grads),
+        6 * rows * width * w_in.shape[1],
+        here,
+        captions,
+        embed_half,
+        w_out,
+        pre_act,
+    )
+    mine = mine + lax.ppermute(other, "core", swap)
+    total = jnp.sum(exchange(mine.astype(BF16), ("y", "xl")).astype(F32), axis=0)
     return total[:share], total[share:]
 
 

time: 153 us -> 148 us (0.967)
  blocking collectives: 131 us -> 119 us
  starting transfers between devices: 9.62 us -> 15.6 us
  Pallas kernels: 1.5 us -> 6.75 us
  matrix products: 3.52 us -> 0 us
  local copies, waits for them, and re-layouts: 5.43 us -> 1.93 us
  waiting for transfers between devices: 0.01 us -> 2.5 us
    all_to_all x5, blocking collectives: 131 us -> 119 us  [exchange(): return lax.all_to_all(x, axes, 0, 0, axis_index_groups=groups, tiled=True)]
    ppermute x1 -> x2, starting transfers between devices: 9.62 us -> 15.6 us  [the longest x1 9.64 us: body(): other_img = lax.ppermute(img, 'core', swap)]
    pallas_call x2 -> x4, Pallas kernels: 1.5 us -> 6.75 us  [call(): pl.pallas_call(kernel, out_shape=outs, in_specs=[pl.BlockSpec(memory_spac...]
    dot_general x4 -> x0, matrix products: 3.52 us -> none  [the longest x1 1.43 us: body(): pre_act = jnp.dot(captions, w_in, preferred_element_type=F32)]
    ppermute x1 -> x2, waiting for transfers between devices: 0.01 us -> 2.5 us  [the longest x1 1.61 us: body(): mine = mine + lax.ppermute(other, 'core', swap)]
    unnamed x12 -> x6, local copies, waits for them, and re-layouts: 1.56 us -> 0.02 us
  transfers between devices with their start and end apart: 1 -> 2, of which waited for: 0 -> 2; matrix products, arithmetic and copies ran while one was open for 1% -> 1% of each run, Pallas kernels for 0% -> 0%
where the time goes in v5:
time: 148 us
  blocking collectives  119 us (80%)
  starting transfers between devices  15.6 us (11%)
  Pallas kernels  6.75 us (5%)
  waiting for transfers between devices  2.5 us (2%)
  local copies, waits for them, and re-layouts  1.93 us (1%)
    all_to_all x5, blocking collectives, exchange(): return lax.all_to_all(x, axes, 0, 0, axis_index_groups=groups, tiled=True)  119 us
    ppermute x1, starting transfers between devices, body(): other_img = lax.ppermute(img, 'core', swap)  9.64 us
    pallas_call x4, Pallas kernels, call(): pl.pallas_call(kernel, out_shape=outs, in_specs=[pl.BlockSpec(memory_spac...  6.75 us
    ppermute x1, starting transfers between devices, body(): mine = mine + lax.ppermute(other, 'core', swap)  6 us
  transfers between devices with their start and end apart: 2, of which 2 were waited for; matrix products, arithmetic and copies ran while one was open for 1% of the time, Pallas kernels for 0%

profile of v5, /device:TPU:1, one launch (start us, length us, event | category | flops | bytes accessed | tf_op | source)
XLA Modules:
  0.0 147.6 jit_solution(12321986427364341836)
XLA Ops:
  0.6 3.8 %shard_map.68 = (bf16[4,144,1152]{2,1,0:T(8,128)(2,1)}, f32[512,128]{1,0:T(8,128)}) custom-call(s32[1]{0:T(128)} %bitcast.core_ref, bf16[512,1152]{1,0:T(8,128)(2,1)} %captions_ref.1, bf16[1152,128]{1,0:T(8,128)(2,1)} %w_in_hbm.1, bf16[128,1152]{1,0:T(8,128)(2,1)} %w_out_ref.1, bf16[32,1152]{1,0:T(8,128)(2,1)} %images_hbm.1), custom_call_target="tpu_custom_call" | custom-call | flops 301989888 | bytes 3000000 | tf_op jit(solution)/shard_map/pallas_call | solution.py:140
  4.4 37.0 %all_to_all.25 = bf16[4,144,1152]{2,1,0:T(8,128)(2,1)S(1)} all-to-all(bf16[4,144,1152]{2,1,0:T(8,128)(2,1)} %get-tuple-element.11), channel_id=1, replica_groups={{0,1,2,3},{4,5,6,7},{8,9,10,11},{12,13,14,15},{16,17,18,19},{20,21,22,2..., dimensions={0} | all-to-all | bytes 2654208 | tf_op jit(solution)/shard_map/all_to_all | solution.py:27
  41.4 0.1 multiply_reduce_fusion
  41.6 0.1 rsqrt.12
  41.7 0.1 fusion
  41.8 0.2 slice_reduce_fusion
  41.9 0.1 broadcast_in_dim.8
  42.1 0.1 pad_maximum_fusion
  42.2 28.3 %all_to_all.26 = bf16[8,80,1152]{2,1,0:T(8,128)(2,1)S(1)} all-to-all(bf16[8,80,1152]{2,1,0:T(8,128)(2,1)S(1)} %pad_maximum_fusion), channel_id=1, replica_groups={{0,4,8,12,16,20,24,28},{1,5,9,13,17,21,25,29},{2,6,10,14,18,22,26,30},{..., dimensions={0} | all-to-all | bytes 2949120 | tf_op jit(solution)/shard_map/all_to_all | solution.py:27
  70.5 0.1 slice.27
  70.7 9.6 %collective-permute-start = (bf16[512,1152]{1,0:T(8,128)(2,1)S(1)}, bf16[512,1152]{1,0:T(8,128)(2,1)S(1)}, u32[]{:S(2)}, u32[]{:S(2)}) collective-permute-start(bf16[512,1152]{1,0:T(8,128)(2,1)S(1)} %bitcast.9), channel_id=1, source_target_pairs={{0,32},{32,0},{1,33},{33,1},{2,34},{34,2},{3,35},{35,3},{4,36},{36... | collective-permute-start | bytes 3538952 | tf_op jit(solution)/shard_map/ppermute | solution.py:195
  80.4 0.8 dynamic_slice.3
  81.1 0.1 broadcast_in_dim.9.pair_ref
  81.2 0.7 shard_map.69
  81.9 0.9 collective-permute-done.img_ref
  82.8 0.8 shard_map.70
  83.6 13.7 %all_to_all.27 = bf16[8,16,1152]{2,1,0:T(8,128)(2,1)S(1)} all-to-all(bf16[8,16,1152]{2,1,0:T(8,128)(2,1)S(1)} %shard_map.70), channel_id=1, replica_groups={{0,4,8,12,16,20,24,28},{1,5,9,13,17,21,25,29},{2,6,10,14,18,22,26,30},{..., dimensions={0} | all-to-all | bytes 589824 | tf_op jit(solution)/shard_map/all_to_all | solution.py:27
  97.2 0.1 broadcast_in_dim.11
  97.3 0.0 copy-start
  97.3 0.0 copy-start.1
  97.4 0.0 copy-start.2
  97.4 22.4 %all_to_all.28 = bf16[4,128,1152]{2,1,0:T(8,128)(2,1)S(1)} all-to-all(bf16[4,128,1152]{2,1,0:T(8,128)(2,1)S(1)} %broadcast_in_dim.11), channel_id=1, replica_groups={{0,1,2,3},{4,5,6,7},{8,9,10,11},{12,13,14,15},{16,17,18,19},{20,21,22,2..., dimensions={0} | all-to-all | bytes 2359296 | tf_op jit(solution)/shard_map/all_to_all | solution.py:27
  119.8 0.0 copy-done
  119.8 0.0 copy-done.1
  119.8 0.0 copy-done.2
  119.8 1.5 %shard_map.71 = (f32[16,72,128]{2,1,0:T(8,128)S(1)}, f32[16,72,128]{2,1,0:T(8,128)S(1)}) custom-call(s32[1]{0:T(128)} %bitcast.core_ref, bf16[512,1152]{1,0:T(8,128)(2,1)S(1)} %copy-done, bf16[512,1152]{1,0:T(8,128)(2,1)S(1)} %bitcast.11, bf16[128,1152]{1,0:T(8,128)(2,1)S(1)} %copy-done.1, f32[512,128]{1,0:T(8,128)S(1)} %copy-done.2), custom_call_target="tpu_custom_call" | custom-call | flops 452984832 | bytes 3000000 | tf_op jit(solution)/shard_map/pallas_call | solution.py:140
  121.3 6.0 %collective-permute-start.1 = (f32[16,72,128]{2,1,0:T(8,128)S(1)}, f32[16,72,128]{2,1,0:T(8,128)S(1)}, u32[]{:S(2)}, u32[]{:S(2)}) collective-permute-start(f32[16,72,128]{2,1,0:T(8,128)S(1)} %get-tuple-element.19), channel_id=1, source_target_pairs={{0,32},{32,0},{1,33},{33,1},{2,34},{34,2},{3,35},{35,3},{4,36},{36... | collective-permute-start | bytes 1769480 | tf_op jit(solution)/shard_map/ppermute | solution.py:238
  127.3 1.6 %collective-permute-done.1 = f32[16,72,128]{2,1,0:T(8,128)S(1)} collective-permute-done((f32[16,72,128]{2,1,0:T(8,128)S(1)}, f32[16,72,128]{2,1,0:T(8,128)S(1)}, u32[]{:S(2)}, u32[]{:S(2)}) %collective-permute-start.1) | collective-permute-done | bytes 589856 | tf_op jit(solution)/shard_map/ppermute | solution.py:238
  129.0 0.1 add_convert_fusion
  129.0 17.9 %all_to_all.29 = bf16[16,72,128]{2,1,0:T(8,128)(2,1)S(1)} all-to-all(bf16[16,72,128]{2,1,0:T(8,128)(2,1)S(1)} %add_convert_fusion), channel_id=1, replica_groups=mesh['y'=8,'xl'=2,'core'=2,'z'=8,'xh'=4] {'y','xl'}, dimensions={0} | all-to-all | bytes 589824 | tf_op jit(solution)/shard_map/all_to_all | solution.py:27
  147.0 0.6 fusion.1
  (4 shorter events, 0.1 us)
Async XLA Ops:
  70.7 12.1 %collective-permute-start = (bf16[512,1152]{1,0:T(8,128)(2,1)S(1)}, bf16[512,1152]{1,0:T(8,128)(2,1)S(1)}, u32[]{:S(2)}, u32[]{:S(2)}) collective-permute-start(bf16[512,1152]{1,0:T(8,128)(2,1)S(1)} %bitcast.9), channel_id=1, source_target_pairs={{0,32},{32,0},{1,33},{33,1},{2,34},{34,2},{3,35},{35,3},{4,36},{36... | collective-permute-start | bytes 3538952 | tf_op jit(solution)/shard_map/ppermute | solution.py:195
  97.3 22.5 %copy-start = (bf16[512,1152]{1,0:T(8,128)(2,1)S(1)}, bf16[512,1152]{1,0:T(8,128)(2,1)}, u32[]{:S(2)}) copy-start(bf16[512,1152]{1,0:T(8,128)(2,1)} %captions_ref.1) | copy-start | bytes 3538948
  97.3 22.5 %copy-start.1 = (bf16[128,1152]{1,0:T(8,128)(2,1)S(1)}, bf16[128,1152]{1,0:T(8,128)(2,1)}, u32[]{:S(2)}) copy-start(bf16[128,1152]{1,0:T(8,128)(2,1)} %w_out_ref.1) | copy-start | bytes 884740
  97.4 22.5 %copy-start.2 = (f32[512,128]{1,0:T(8,128)S(1)}, f32[512,128]{1,0:T(8,128)}, u32[]{:S(2)}) copy-start(f32[512,128]{1,0:T(8,128)} %get-tuple-element.17.pre_ref) | copy-start | bytes 786436
  121.3 7.6 %collective-permute-start.1 = (f32[16,72,128]{2,1,0:T(8,128)S(1)}, f32[16,72,128]{2,1,0:T(8,128)S(1)}, u32[]{:S(2)}, u32[]{:S(2)}) collective-permute-start(f32[16,72,128]{2,1,0:T(8,128)S(1)} %get-tuple-element.19), channel_id=1, source_target_pairs={{0,32},{32,0},{1,33},{33,1},{2,34},{34,2},{3,35},{35,3},{4,36},{36... | collective-permute-start | bytes 1769480 | tf_op jit(solution)/shard_map/ppermute | solution.py:238

commit v6 on v5

--- a/solution.py
+++ b/solution.py
@@ -54,16 +54,17 @@
     per_first, img_part, core_ref, captions_hbm, w_in_hbm, w_out_hbm, images_hbm, out_hbm, pre_hbm,
     captions_ref, w_in_ref, w_out_ref, img_ref, out_ref, pre_ref, sems
 ):
-    n = out_ref.shape[0]
+    n = out_ref.shape[0] // 2
+    half = n * per_first
     start = pl.multiple_of(core_ref[0] * img_part, img_part)
-    blocks = [pl.ds(k * per_first, per_first) for k in range(n)]
     fetch_in = pltpu.make_async_copy(w_in_hbm, w_in_ref, sems.at[0])
     fetch_out = pltpu.make_async_copy(w_out_hbm, w_out_ref, sems.at[1])
     fetch_img = pltpu.make_async_copy(images_hbm.at[pl.ds(start, img_part)], img_ref, sems.at[2])
+    blocks = [pl.ds(k * half, half) for k in range(2)]
     fetches = [
         pltpu.make_async_copy(captions_hbm.at[at], captions_ref.at[at], sems.at[3 + k]) for k, at in enumerate(blocks)
     ]
-    for copy in (fetch_in, fetches[0], fetch_out, fetch_img, *fetches[1:]):
+    for copy in (fetch_in, fetches[0], fetch_out, fetch_img, fetches[1]):
         copy.start()
     stores = []
     fetch_in.wait()
@@ -75,10 +76,13 @@
         if k == 0:
             fetch_out.wait()
             fetch_img.wait()
-        out_ref[k, :per_first] = jnp.dot(hidden, w_out_ref[...], preferred_element_type=F32).astype(BF16)
-        out_ref[k, per_first:] = img_ref[...]
-        stores.append(pltpu.make_async_copy(out_ref.at[k], out_hbm.at[k], sems.at[3 + n + k]))
-        stores.append(pltpu.make_async_copy(pre_ref.at[at], pre_hbm.at[at], sems.at[3 + 2 * n + k]))
+        total = jnp.dot(hidden, w_out_ref[...], preferred_element_type=F32).astype(BF16)
+        for q in range(n):
+            out_ref[k * n + q, :per_first] = total[q * per_first : (q + 1) * per_first]
+            out_ref[k * n + q, per_first:] = img_ref[...]
+        to = pl.ds(k * n, n)
+        stores.append(pltpu.make_async_copy(out_ref.at[to], out_hbm.at[to], sems.at[5 + k]))
+        stores.append(pltpu.make_async_copy(pre_ref.at[at], pre_hbm.at[at], sems.at[7 + k]))
         stores[-2].start()
         stores[-1].start()
     for copy in stores:
@@ -102,7 +106,7 @@
             even = grad[2 * q * share : (2 * q + 1) * share]
             odd = grad[(2 * q + 1) * share : (2 * q + 2) * share]
             mine_ref[q, at : at + share] = jnp.where(zero, even, odd)
-            other_ref[q, at : at + share] = jnp.where(zero, odd, even)
+            other_ref[q, at : at + share] = jnp.where(zero, odd, even).astype(BF16)
 
 
 def half_grad(core, geometry, unit_half, pair, img):
@@ -181,7 +185,7 @@
             pltpu.VMEM((img_part, width), BF16),
             pltpu.VMEM(sums.shape, BF16),
             pltpu.VMEM(acts.shape, F32),
-            pltpu.SemaphoreType.DMA((3 + 3 * n_xh,)),
+            pltpu.SemaphoreType.DMA((9,)),
         ],
     )
     got = exchange(sent, CHIPS, first)
@@ -224,10 +228,10 @@
     embed_half = exchange(to_all(got, n_xh), CHIPS, first).reshape(rows, width)
 
     share = width // n_dp
-    grads = jax.ShapeDtypeStruct((n_dp // n_core, 2 * share, w_in.shape[1]), F32)
+    grads = (n_dp // n_core, 2 * share, w_in.shape[1])
     mine, other = call(
         functools.partial(backward_kernel, share),
-        (grads, grads),
+        (jax.ShapeDtypeStruct(grads, F32), jax.ShapeDtypeStruct(grads, BF16)),
         6 * rows * width * w_in.shape[1],
         here,
         captions,
@@ -235,7 +239,7 @@
         w_out,
         pre_act,
     )
-    mine = mine + lax.ppermute(other, "core", swap)
+    mine = mine + lax.ppermute(other, "core", swap).astype(F32)
     total = jnp.sum(exchange(mine.astype(BF16), ("y", "xl")).astype(F32), axis=0)
     return total[:share], total[share:]
 

time: 148 us -> 147 us (level)
  no operation moved by 1% of the time
where the time goes in v6:
time: 147 us
  blocking collectives  120 us (82%)
  starting transfers between devices  15.4 us (10%)
  Pallas kernels  6.36 us (4%)
  waiting for transfers between devices  2.08 us (1%)
  local copies, waits for them, and re-layouts  1.93 us (1%)
    all_to_all x5, blocking collectives, exchange(): return lax.all_to_all(x, axes, 0, 0, axis_index_groups=groups, tiled=True)  120 us
    ppermute x1, starting transfers between devices, body(): other_img = lax.ppermute(img, 'core', swap)  9.64 us
    pallas_call x4, Pallas kernels, call(): pl.pallas_call(kernel, out_shape=outs, in_specs=[pl.BlockSpec(memory_spac...  6.36 us
    ppermute x1, starting transfers between devices, body(): mine = mine + lax.ppermute(other, 'core', swap).astype(F32)  5.74 us
  transfers between devices with their start and end apart: 2, of which 2 were waited for; matrix products, arithmetic and copies ran while one was open for 1% of the time, Pallas kernels for 0%

profile of v6, /device:TPU:1, one launch (start us, length us, event | category | flops | bytes accessed | tf_op | source)
XLA Modules:
  0.0 146.7 jit_solution(14204838182155722224)
XLA Ops:
  0.6 3.4 %shard_map.68 = (bf16[4,144,1152]{2,1,0:T(8,128)(2,1)}, f32[512,128]{1,0:T(8,128)}) custom-call(s32[1]{0:T(128)} %bitcast.core_ref, bf16[512,1152]{1,0:T(8,128)(2,1)} %captions_ref.1, bf16[1152,128]{1,0:T(8,128)(2,1)} %w_in_hbm.1, bf16[128,1152]{1,0:T(8,128)(2,1)} %w_out_ref.1, bf16[32,1152]{1,0:T(8,128)(2,1)} %images_hbm.1), custom_call_target="tpu_custom_call" | custom-call | flops 301989888 | bytes 3000000 | tf_op jit(solution)/shard_map/pallas_call | solution.py:144
  4.0 37.0 %all_to_all.25 = bf16[4,144,1152]{2,1,0:T(8,128)(2,1)S(1)} all-to-all(bf16[4,144,1152]{2,1,0:T(8,128)(2,1)} %get-tuple-element.11), channel_id=1, replica_groups={{0,1,2,3},{4,5,6,7},{8,9,10,11},{12,13,14,15},{16,17,18,19},{20,21,22,2..., dimensions={0} | all-to-all | bytes 2654208 | tf_op jit(solution)/shard_map/all_to_all | solution.py:27
  41.1 0.1 multiply_reduce_fusion
  41.2 0.1 rsqrt.12
  41.3 0.1 fusion
  41.4 0.2 slice_reduce_fusion
  41.5 0.1 broadcast_in_dim.8
  41.7 0.1 pad_maximum_fusion
  41.8 28.3 %all_to_all.26 = bf16[8,80,1152]{2,1,0:T(8,128)(2,1)S(1)} all-to-all(bf16[8,80,1152]{2,1,0:T(8,128)(2,1)S(1)} %pad_maximum_fusion), channel_id=1, replica_groups={{0,4,8,12,16,20,24,28},{1,5,9,13,17,21,25,29},{2,6,10,14,18,22,26,30},{..., dimensions={0} | all-to-all | bytes 2949120 | tf_op jit(solution)/shard_map/all_to_all | solution.py:27
  70.2 0.1 slice.27
  70.3 9.6 %collective-permute-start = (bf16[512,1152]{1,0:T(8,128)(2,1)S(1)}, bf16[512,1152]{1,0:T(8,128)(2,1)S(1)}, u32[]{:S(2)}, u32[]{:S(2)}) collective-permute-start(bf16[512,1152]{1,0:T(8,128)(2,1)S(1)} %bitcast.9), channel_id=1, source_target_pairs={{0,32},{32,0},{1,33},{33,1},{2,34},{34,2},{3,35},{35,3},{4,36},{36... | collective-permute-start | bytes 3538952 | tf_op jit(solution)/shard_map/ppermute | solution.py:199
  80.0 0.8 dynamic_slice.3
  80.8 0.1 broadcast_in_dim.9.pair_ref
  80.8 0.7 shard_map.69
  81.5 0.9 collective-permute-done.img_ref
  82.4 0.8 shard_map.70
  83.2 13.7 %all_to_all.27 = bf16[8,16,1152]{2,1,0:T(8,128)(2,1)S(1)} all-to-all(bf16[8,16,1152]{2,1,0:T(8,128)(2,1)S(1)} %shard_map.70), channel_id=1, replica_groups={{0,4,8,12,16,20,24,28},{1,5,9,13,17,21,25,29},{2,6,10,14,18,22,26,30},{..., dimensions={0} | all-to-all | bytes 589824 | tf_op jit(solution)/shard_map/all_to_all | solution.py:27
  96.9 0.1 broadcast_in_dim.11
  97.0 0.0 copy-start
  97.0 0.0 copy-start.1
  97.0 0.0 copy-start.2
  97.0 22.6 %all_to_all.28 = bf16[4,128,1152]{2,1,0:T(8,128)(2,1)S(1)} all-to-all(bf16[4,128,1152]{2,1,0:T(8,128)(2,1)S(1)} %broadcast_in_dim.11), channel_id=1, replica_groups={{0,1,2,3},{4,5,6,7},{8,9,10,11},{12,13,14,15},{16,17,18,19},{20,21,22,2..., dimensions={0} | all-to-all | bytes 2359296 | tf_op jit(solution)/shard_map/all_to_all | solution.py:27
  119.6 0.0 copy-done
  119.6 0.0 copy-done.1
  119.6 0.0 copy-done.2
  119.6 1.5 %shard_map.71 = (f32[16,72,128]{2,1,0:T(8,128)S(1)}, bf16[16,72,128]{2,1,0:T(8,128)(2,1)S(1)}) custom-call(s32[1]{0:T(128)} %bitcast.core_ref, bf16[512,1152]{1,0:T(8,128)(2,1)S(1)} %copy-done, bf16[512,1152]{1,0:T(8,128)(2,1)S(1)} %bitcast.11, bf16[128,1152]{1,0:T(8,128)(2,1)S(1)} %copy-done.1, f32[512,128]{1,0:T(8,128)S(1)} %copy-done.2), custom_call_target="tpu_custom_call" | custom-call | flops 452984832 | bytes 3000000 | tf_op jit(solution)/shard_map/pallas_call | solution.py:144
  121.1 5.7 %collective-permute-start.1 = (bf16[16,72,128]{2,1,0:T(8,128)(2,1)S(1)}, bf16[16,72,128]{2,1,0:T(8,128)(2,1)S(1)}, u32[]{:S(2)}, u32[]{:S(2)}) collective-permute-start(bf16[16,72,128]{2,1,0:T(8,128)(2,1)S(1)} %get-tuple-element.19), channel_id=1, source_target_pairs={{0,32},{32,0},{1,33},{33,1},{2,34},{34,2},{3,35},{35,3},{4,36},{36... | collective-permute-start | bytes 884744 | tf_op jit(solution)/shard_map/ppermute | solution.py:242
  126.9 1.2 collective-permute-done.1
  128.1 0.1 add_convert_fusion
  128.1 17.9 %all_to_all.29 = bf16[16,72,128]{2,1,0:T(8,128)(2,1)S(1)} all-to-all(bf16[16,72,128]{2,1,0:T(8,128)(2,1)S(1)} %add_convert_fusion), channel_id=1, replica_groups=mesh['y'=8,'xl'=2,'core'=2,'z'=8,'xh'=4] {'y','xl'}, dimensions={0} | all-to-all | bytes 589824 | tf_op jit(solution)/shard_map/all_to_all | solution.py:27
  146.1 0.6 fusion.1
  (4 shorter events, 0.1 us)
Async XLA Ops:
  70.3 12.1 %collective-permute-start = (bf16[512,1152]{1,0:T(8,128)(2,1)S(1)}, bf16[512,1152]{1,0:T(8,128)(2,1)S(1)}, u32[]{:S(2)}, u32[]{:S(2)}) collective-permute-start(bf16[512,1152]{1,0:T(8,128)(2,1)S(1)} %bitcast.9), channel_id=1, source_target_pairs={{0,32},{32,0},{1,33},{33,1},{2,34},{34,2},{3,35},{35,3},{4,36},{36... | collective-permute-start | bytes 3538952 | tf_op jit(solution)/shard_map/ppermute | solution.py:199
  97.0 22.7 %copy-start = (bf16[512,1152]{1,0:T(8,128)(2,1)S(1)}, bf16[512,1152]{1,0:T(8,128)(2,1)}, u32[]{:S(2)}) copy-start(bf16[512,1152]{1,0:T(8,128)(2,1)} %captions_ref.1) | copy-start | bytes 3538948
  97.0 22.6 %copy-start.1 = (bf16[128,1152]{1,0:T(8,128)(2,1)S(1)}, bf16[128,1152]{1,0:T(8,128)(2,1)}, u32[]{:S(2)}) copy-start(bf16[128,1152]{1,0:T(8,128)(2,1)} %w_out_ref.1) | copy-start | bytes 884740
  97.0 22.6 %copy-start.2 = (f32[512,128]{1,0:T(8,128)S(1)}, f32[512,128]{1,0:T(8,128)}, u32[]{:S(2)}) copy-start(f32[512,128]{1,0:T(8,128)} %get-tuple-element.17.pre_ref) | copy-start | bytes 786436
  121.1 6.9 %collective-permute-start.1 = (bf16[16,72,128]{2,1,0:T(8,128)(2,1)S(1)}, bf16[16,72,128]{2,1,0:T(8,128)(2,1)S(1)}, u32[]{:S(2)}, u32[]{:S(2)}) collective-permute-start(bf16[16,72,128]{2,1,0:T(8,128)(2,1)S(1)} %get-tuple-element.19), channel_id=1, source_target_pairs={{0,32},{32,0},{1,33},{33,1},{2,34},{34,2},{3,35},{35,3},{4,36},{36... | collective-permute-start | bytes 884744 | tf_op jit(solution)/shard_map/ppermute | solution.py:242

commit v7 on v6

--- a/solution.py
+++ b/solution.py
@@ -16,6 +16,7 @@
 SCALE = 10.0
 BIAS = -5.0
 EPS = 1e-06
+DIGIT = 32
 CURVE = math.sqrt(2.0 / math.pi)
 CUBIC = 0.044715
 GRANT = 60 * 1024 * 1024
@@ -51,12 +52,12 @@
 
 
 def forward_kernel(
-    per_first, img_part, core_ref, captions_hbm, w_in_hbm, w_out_hbm, images_hbm, out_hbm, pre_hbm,
+    per_first, img_part, where, captions_hbm, w_in_hbm, w_out_hbm, images_hbm, out_hbm, pre_hbm,
     captions_ref, w_in_ref, w_out_ref, img_ref, out_ref, pre_ref, sems
 ):
     n = out_ref.shape[0] // 2
     half = n * per_first
-    start = pl.multiple_of(core_ref[0] * img_part, img_part)
+    start = pl.multiple_of(where[0] * img_part, img_part)
     fetch_in = pltpu.make_async_copy(w_in_hbm, w_in_ref, sems.at[0])
     fetch_out = pltpu.make_async_copy(w_out_hbm, w_out_ref, sems.at[1])
     fetch_img = pltpu.make_async_copy(images_hbm.at[pl.ds(start, img_part)], img_ref, sems.at[2])
@@ -89,7 +90,7 @@
         copy.wait()
 
 
-def backward_kernel(share, core_ref, captions_ref, embed_ref, w_out_ref, pre_ref, mine_ref, other_ref):
+def backward_kernel(share, where, captions_ref, embed_ref, w_out_ref, pre_ref, mine_ref, other_ref):
     embed_half = embed_ref[...]
     hidden_grad = lax.dot_general(embed_half, w_out_ref[...], (((1,), (1,)), ((), ())), preferred_element_type=F32)
     v = pre_ref[...]
@@ -100,7 +101,7 @@
     over_rows = (((0,), (0,)), ((), ()))
     grad_in = lax.dot_general(preact_grad, captions_ref[...], over_rows, preferred_element_type=F32).T
     grad_out = lax.dot_general(hidden, embed_half, over_rows, preferred_element_type=F32).T
-    zero = core_ref[0] == 0
+    zero = where[0] % 2 == 0
     for at, grad in ((0, grad_in), (share, grad_out)):
         for q in range(mine_ref.shape[0]):
             even = grad[2 * q * share : (2 * q + 1) * share]
@@ -109,30 +110,45 @@
             other_ref[q, at : at + share] = jnp.where(zero, odd, even).astype(BF16)
 
 
-def half_grad(core, geometry, unit_half, pair, img):
+def half_grad(spot, geometry, unit_half, pair, img):
     n_z, n_xh, img_block, img_part = geometry
     n = lax.broadcasted_iota(jnp.int32, (1, img.shape[0]), 1)
     slot, row = n // img_part, n % img_part
-    block = jnp.where(core == 0, slot, (slot % n_xh) * n_z + slot // n_xh)
+    block = jnp.where(spot % 2 == 0, slot, (slot % n_xh) * n_z + slot // n_xh)
     logits = SCALE * lax.dot_general(unit_half, img, (((1,), (1,)), ((), ())), preferred_element_type=F32) + BIAS
-    label = (pair == block * img_block + core * img_part + row).astype(F32)
-    mismatch = (jax.nn.sigmoid(logits) - label).astype(BF16)
+    column = block * img_block + spot * img_part + row
+    mismatch = (jax.nn.sigmoid(logits) - (pair == column).astype(F32)).astype(BF16)
     return jnp.dot(mismatch, img, preferred_element_type=F32)
 
 
-def own_kernel(geometry, core_ref, sum_ref, pair_ref, img_ref, dir_ref, norm_ref, grad_ref):
+def norm_kernel(where, sum_ref, pair_ref, dir_ref, norm_ref, unit_ref):
     embedding = sum_ref[...]
+    width = embedding.shape[1]
     inv_norm = lax.rsqrt(jnp.sum(embedding * embedding, axis=1, keepdims=True) + EPS)
     unit_dir = embedding * inv_norm
     dir_ref[...] = unit_dir
     norm_ref[...] = jnp.broadcast_to(inv_norm, norm_ref.shape)
-    grad_ref[...] = half_grad(core_ref[0], geometry, unit_dir.astype(BF16), pair_ref[:, :1], img_ref[...])
-
-
-def other_kernel(geometry, core_ref, dir_ref, norm_ref, grad_ref, pair_ref, img_ref, out_ref):
+    pair = pair_ref[...]
+    lane = lax.broadcasted_iota(jnp.int32, pair.shape, 1)
+    digits = jnp.where(lane == 0, pair // DIGIT, jnp.where(lane == 1, pair % DIGIT, 0))
+    unit_ref[:, :width] = unit_dir.astype(BF16)
+    unit_ref[:, width:] = digits.astype(F32).astype(BF16)
+
+
+def score_kernel(geometry, where, unit_ref, mine_ref, other_ref, grad_ref):
+    width = grad_ref.shape[1]
+    spot = where[0]
+    digits = unit_ref[:, width:].astype(F32)
+    pair = (digits[:, :1] * DIGIT + digits[:, 1:2]).astype(jnp.int32)
+    unit_half = unit_ref[:, :width]
+    grad_ref[...] = half_grad(spot, geometry, unit_half, pair, mine_ref[...]) + half_grad(
+        spot + 1 - 2 * (spot % 2), geometry, unit_half, pair, other_ref[...]
+    )
+
+
+def project_kernel(where, dir_ref, norm_ref, mine_ref, other_ref, out_ref):
     unit_dir = dir_ref[...]
-    more = half_grad(1 - core_ref[0], geometry, unit_dir.astype(BF16), pair_ref[:, :1], img_ref[...])
-    unit_grad = SCALE * (grad_ref[...] + more)
+    unit_grad = SCALE * (mine_ref[...] + other_ref[...])
     along = jnp.sum(unit_dir * unit_grad, axis=1, keepdims=True)
     embed_half = ((unit_grad - unit_dir * along) * norm_ref[:, :1]).astype(BF16)
     for k in range(out_ref.shape[0]):
@@ -162,9 +178,9 @@
     per_first = rows // n_xh
     own = per_first // n_z
     img_block = images.shape[0]
-    img_part = img_block // n_core
-
-    here = core.reshape(1).astype(jnp.int32)
+    img_part = img_block // (n_core * lax.axis_size("xl"))
+
+    here = lax.axis_index(("xl", "core")).reshape(1).astype(jnp.int32)
     sums = jax.ShapeDtypeStruct((n_xh, per_first + img_part, width), BF16)
     acts = jax.ShapeDtypeStruct((rows, w_in.shape[1]), F32)
     sent, pre_act = call(
@@ -196,33 +212,36 @@
     got = exchange(sent, CHIPS, second)
     embedding = jnp.sum(got[:, :own].astype(F32), axis=0)
     embedding, img = lax.optimization_barrier((embedding, got[:, own:].reshape(-1, width)))
-    other_img = lax.ppermute(img, "core", swap)
 
     at_first, at_second = place(core, n_z, n_xh, lax.axis_index("z"), lax.axis_index("xh"))
     pair = lax.dynamic_slice_in_dim(pairs, at_first * per_first + at_second * own, own, 0)
     pair = jnp.broadcast_to(pair[:, None], (own, 128))
-    geometry = (n_z, n_xh, img_block, img_part)
-    flops = 4 * own * img.shape[0] * width
     row = jax.ShapeDtypeStruct((own, width), F32)
-    unit_dir, inv_norm, grad = call(
-        functools.partial(own_kernel, geometry),
-        (row, jax.ShapeDtypeStruct((own, 128), F32), row),
-        flops,
+    unit_dir, inv_norm, unit = call(
+        norm_kernel,
+        (row, jax.ShapeDtypeStruct((own, 128), F32), jax.ShapeDtypeStruct((own, width + 128), BF16)),
+        own * width,
         here,
         embedding,
         pair,
-        img,
-    )
+    )
+    unit, img = lax.optimization_barrier((unit, img))
+    other_img = lax.ppermute(img, "core", swap)
+    other_unit = lax.ppermute(unit, "xl", swap)
+    score = functools.partial(score_kernel, (n_z, n_xh, img_block, img_part))
+    flops = 8 * own * img.shape[0] * width
+    grad = call(score, row, flops, here, unit, img, other_img)
+    other_grad = call(score, row, flops, here, other_unit, img, other_img)
+    other_grad = lax.ppermute(other_grad, "xl", swap)
     sent = call(
-        functools.partial(other_kernel, geometry),
+        project_kernel,
         jax.ShapeDtypeStruct((n_z, own, width), BF16),
-        flops,
+        own * width,
         here,
         unit_dir,
         inv_norm,
         grad,
-        pair,
-        other_img,
+        other_grad,
     )
     got = exchange(sent, CHIPS, second).reshape(per_first, width)
     embed_half = exchange(to_all(got, n_xh), CHIPS, first).reshape(rows, width)

time: 147 us -> 146 us (level)
  blocking collectives: 120 us -> 89 us
  waiting for transfers between devices: 2.08 us -> 18.7 us
  starting transfers between devices: 15.4 us -> 27.4 us
    all_to_all x5 -> x4, blocking collectives: 120 us -> 89 us  [exchange(): return lax.all_to_all(x, axes, 0, 0, axis_index_groups=groups, tiled=True)]
    all_to_all x0 -> x1, waiting for transfers between devices: none -> 14.4 us  [exchange(): return lax.all_to_all(x, axes, 0, 0, axis_index_groups=groups, tiled=True)]
    all_to_all x0 -> x1, starting transfers between devices: none -> 6.68 us  [exchange(): return lax.all_to_all(x, axes, 0, 0, axis_index_groups=groups, tiled=True)]
    ppermute x0 -> x2, starting transfers between devices: none -> 6.46 us  [the longest x1 3.46 us: body(): other_unit = lax.ppermute(unit, 'xl', swap)]
    ppermute x0 -> x2, waiting for transfers between devices: none -> 3.15 us  [the longest x1 1.73 us: body(): other_unit = lax.ppermute(unit, 'xl', swap)]
    pallas_call x4 -> x6, Pallas kernels: 6.36 us -> 6.46 us  [call(): pl.pallas_call(kernel, out_shape=outs, in_specs=[pl.BlockSpec(memory_spac...]
  transfers between devices with their start and end apart: 2 -> 5, of which waited for: 2 -> 4; matrix products, arithmetic and copies ran while one was open for 1% -> 1% of each run, Pallas kernels for 0% -> 0%
where the time goes in v7:
time: 146 us
  blocking collectives  89 us (61%)
  starting transfers between devices  27.4 us (19%)
  waiting for transfers between devices  18.7 us (13%)
  Pallas kernels  6.46 us (4%)
  local copies, waits for them, and re-layouts  1.72 us (1%)
  other arithmetic  1.48 us (1%)
    all_to_all x4, blocking collectives, exchange(): return lax.all_to_all(x, axes, 0, 0, axis_index_groups=groups, tiled=True)  89 us
    all_to_all x1, waiting for transfers between devices, exchange(): return lax.all_to_all(x, axes, 0, 0, axis_index_groups=groups, tiled=True)  14.4 us
    ppermute x1, starting transfers between devices, body(): other_img = lax.ppermute(img, 'core', swap)  8.31 us
    all_to_all x1, starting transfers between devices, exchange(): return lax.all_to_all(x, axes, 0, 0, axis_index_groups=groups, tiled=True)  6.68 us
    pallas_call x6, Pallas kernels, call(): pl.pallas_call(kernel, out_shape=outs, in_specs=[pl.BlockSpec(memory_spac...  6.46 us
    ppermute x1, starting transfers between devices, body(): mine = mine + lax.ppermute(other, 'core', swap).astype(F32)  5.96 us
    ppermute x1, starting transfers between devices, body(): other_unit = lax.ppermute(unit, 'xl', swap)  3.46 us
    ppermute x1, starting transfers between devices, body(): other_grad = lax.ppermute(other_grad, 'xl', swap)  3 us
  transfers between devices with their start and end apart: 5, of which 4 were waited for; matrix products, arithmetic and copies ran while one was open for 1% of the time, Pallas kernels for 0%

profile of v7, /device:TPU:1, one launch (start us, length us, event | category | flops | bytes accessed | tf_op | source)
XLA Modules:
  0.0 145.6 jit_solution(16722860153675077836)
XLA Ops:
  0.6 3.4 %shard_map.68 = (bf16[4,136,1152]{2,1,0:T(8,128)(2,1)}, f32[512,128]{1,0:T(8,128)}) custom-call(s32[1]{0:T(128)} %bitcast.where, bf16[512,1152]{1,0:T(8,128)(2,1)} %captions_ref.1, bf16[1152,128]{1,0:T(8,128)(2,1)} %w_in_hbm.1, bf16[128,1152]{1,0:T(8,128)(2,1)} %w_out_ref.1, bf16[32,1152]{1,0:T(8,128)(2,1)} %images_hbm.1), custom_call_target="tpu_custom_call" | custom-call | flops 301989888 | bytes 3000000 | tf_op jit(solution)/shard_map/pallas_call | solution.py:160
  4.1 36.1 %all_to_all.25 = bf16[4,136,1152]{2,1,0:T(8,128)(2,1)S(1)} all-to-all(bf16[4,136,1152]{2,1,0:T(8,128)(2,1)} %get-tuple-element.13), channel_id=1, replica_groups={{0,1,2,3},{4,5,6,7},{8,9,10,11},{12,13,14,15},{16,17,18,19},{20,21,22,2..., dimensions={0} | all-to-all | bytes 2506752 | tf_op jit(solution)/shard_map/all_to_all | solution.py:28
  40.1 0.1 fusion.2
  40.2 0.1 rsqrt.12
  40.3 0.2 slice_reduce_fusion
  40.5 0.1 fusion.1
  40.6 1.0 pad_maximum_fusion
  41.6 6.7 %all-to-all-start.1 = ((bf16[8,48,1152]{2,1,0:T(8,128)(2,1)}), bf16[8,48,1152]{2,1,0:T(8,128)(2,1)S(1)}, u32[]{:S(2)}, u32[]{:S(2)}) async-start(bf16[8,48,1152]{2,1,0:T(8,128)(2,1)} %pad_maximum_fusion), calls=%async_computation.1 | async-start | bytes 1769472 | tf_op jit(solution)/shard_map/all_to_all | solution.py:28
  48.3 0.8 dynamic_slice.3
  49.0 14.4 %all-to-all-done.1 = bf16[8,48,1152]{2,1,0:T(8,128)(2,1)S(1)} async-done(((bf16[8,48,1152]{2,1,0:T(8,128)(2,1)}), bf16[8,48,1152]{2,1,0:T(8,128)(2,1)S(1)}, u32[]{:S(2)}, u32[]{:S(2)}) %all-to-all-start.1) | async-done | bytes 884768 | tf_op jit(solution)/shard_map/all_to_all | solution.py:28
  63.5 0.1 broadcast_in_dim.9.pair_ref
  63.6 0.1 shard_map.69
  63.7 8.3 %collective-permute-start = (bf16[256,1152]{1,0:T(8,128)(2,1)S(1)}, bf16[256,1152]{1,0:T(8,128)(2,1)S(1)}, u32[]{:S(2)}, u32[]{:S(2)}) collective-permute-start(bf16[256,1152]{1,0:T(8,128)(2,1)S(1)} %bitcast.11), channel_id=1, source_target_pairs={{0,32},{32,0},{1,33},{33,1},{2,34},{34,2},{3,35},{35,3},{4,36},{36... | collective-permute-start | bytes 1769480 | tf_op jit(solution)/shard_map/ppermute | solution.py:229
  72.0 3.5 %collective-permute-start.1 = (bf16[16,1280]{1,0:T(8,128)(2,1)S(1)}, bf16[16,1280]{1,0:T(8,128)(2,1)S(1)}, u32[]{:S(2)}, u32[]{:S(2)}) collective-permute-start(bf16[16,1280]{1,0:T(8,128)(2,1)S(1)} %get-tuple-element.19.unit_ref), channel_id=1, source_target_pairs={{0,64},{64,0},{1,65},{65,1},{2,66},{66,2},{3,67},{67,3},{4,68},{68... | collective-permute-start | bytes 122888 | tf_op jit(solution)/shard_map/ppermute | solution.py:230
  75.5 1.7 %collective-permute-done.1.unit_ref = bf16[16,1280]{1,0:T(8,128)(2,1)S(1)} collective-permute-done((bf16[16,1280]{1,0:T(8,128)(2,1)S(1)}, bf16[16,1280]{1,0:T(8,128)(2,1)S(1)}, u32[]{:S(2)}, u32[]{:S(2)}) %collective-permute-start.1) | collective-permute-done | bytes 40992 | tf_op jit(solution)/shard_map/ppermute | solution.py:230
  77.2 0.0 collective-permute-done.other_ref
  77.2 0.7 shard_map.71
  77.9 3.0 %collective-permute-start.2 = (f32[16,1152]{1,0:T(8,128)S(1)}, f32[16,1152]{1,0:T(8,128)S(1)}, u32[]{:S(2)}, u32[]{:S(2)}) collective-permute-start(f32[16,1152]{1,0:T(8,128)S(1)} %shard_map.71), channel_id=1, source_target_pairs={{0,64},{64,0},{1,65},{65,1},{2,66},{66,2},{3,67},{67,3},{4,68},{68... | collective-permute-start | bytes 221192 | tf_op jit(solution)/shard_map/ppermute | solution.py:235
  80.9 0.7 shard_map.70.mine_ref
  81.5 1.4 collective-permute-done.2.other_ref
  83.0 0.1 shard_map.72
  83.1 12.7 %all_to_all.26 = bf16[8,16,1152]{2,1,0:T(8,128)(2,1)S(1)} all-to-all(bf16[8,16,1152]{2,1,0:T(8,128)(2,1)S(1)} %shard_map.72), channel_id=1, replica_groups={{0,4,8,12,16,20,24,28},{1,5,9,13,17,21,25,29},{2,6,10,14,18,22,26,30},{..., dimensions={0} | all-to-all | bytes 589824 | tf_op jit(solution)/shard_map/all_to_all | solution.py:28
  95.8 0.1 broadcast_in_dim.11
  95.9 0.0 copy-start
  95.9 0.0 copy-start.1
  95.9 21.5 %all_to_all.27 = bf16[4,128,1152]{2,1,0:T(8,128)(2,1)S(1)} all-to-all(bf16[4,128,1152]{2,1,0:T(8,128)(2,1)S(1)} %broadcast_in_dim.11), channel_id=1, replica_groups={{0,1,2,3},{4,5,6,7},{8,9,10,11},{12,13,14,15},{16,17,18,19},{20,21,22,2..., dimensions={0} | all-to-all | bytes 2359296 | tf_op jit(solution)/shard_map/all_to_all | solution.py:28
  117.4 1.5 %shard_map.73 = (f32[16,72,128]{2,1,0:T(8,128)S(1)}, bf16[16,72,128]{2,1,0:T(8,128)(2,1)S(1)}) custom-call(s32[1]{0:T(128)} %bitcast.where, bf16[512,1152]{1,0:T(8,128)(2,1)S(1)} %copy-done, bf16[512,1152]{1,0:T(8,128)(2,1)S(1)} %bitcast.14, bf16[128,1152]{1,0:T(8,128)(2,1)S(1)} %copy-done.1, f32[512,128]{1,0:T(8,128)S(1)} %copy-done.2), custom_call_target="tpu_custom_call" | custom-call | flops 452984832 | bytes 3000000 | tf_op jit(solution)/shard_map/pallas_call | solution.py:160
  118.9 6.0 %collective-permute-start.3 = (bf16[16,72,128]{2,1,0:T(8,128)(2,1)S(1)}, bf16[16,72,128]{2,1,0:T(8,128)(2,1)S(1)}, u32[]{:S(2)}, u32[]{:S(2)}) collective-permute-start(bf16[16,72,128]{2,1,0:T(8,128)(2,1)S(1)} %get-tuple-element.23), channel_id=1, source_target_pairs={{0,32},{32,0},{1,33},{33,1},{2,34},{34,2},{3,35},{35,3},{4,36},{36... | collective-permute-start | bytes 884744 | tf_op jit(solution)/shard_map/ppermute | solution.py:261
  124.9 1.2 collective-permute-done.3
  126.1 0.1 add_convert_fusion
  126.2 18.7 %all_to_all.28 = bf16[16,72,128]{2,1,0:T(8,128)(2,1)S(1)} all-to-all(bf16[16,72,128]{2,1,0:T(8,128)(2,1)S(1)} %add_convert_fusion), channel_id=1, replica_groups=mesh['y'=8,'xl'=2,'core'=2,'z'=8,'xh'=4] {'y','xl'}, dimensions={0} | all-to-all | bytes 589824 | tf_op jit(solution)/shard_map/all_to_all | solution.py:28
  144.9 0.6 fusion.3
  (9 shorter events, 0.2 us)
Async XLA Ops:
  41.6 21.8 %all-to-all-start.1 = ((bf16[8,48,1152]{2,1,0:T(8,128)(2,1)}), bf16[8,48,1152]{2,1,0:T(8,128)(2,1)S(1)}, u32[]{:S(2)}, u32[]{:S(2)}) async-start(bf16[8,48,1152]{2,1,0:T(8,128)(2,1)} %pad_maximum_fusion), calls=%async_computation.1 | async-start | bytes 1769472 | tf_op jit(solution)/shard_map/all_to_all | solution.py:28
  63.7 13.5 %collective-permute-start = (bf16[256,1152]{1,0:T(8,128)(2,1)S(1)}, bf16[256,1152]{1,0:T(8,128)(2,1)S(1)}, u32[]{:S(2)}, u32[]{:S(2)}) collective-permute-start(bf16[256,1152]{1,0:T(8,128)(2,1)S(1)} %bitcast.11), channel_id=1, source_target_pairs={{0,32},{32,0},{1,33},{33,1},{2,34},{34,2},{3,35},{35,3},{4,36},{36... | collective-permute-start | bytes 1769480 | tf_op jit(solution)/shard_map/ppermute | solution.py:229
  72.0 5.2 %collective-permute-start.1 = (bf16[16,1280]{1,0:T(8,128)(2,1)S(1)}, bf16[16,1280]{1,0:T(8,128)(2,1)S(1)}, u32[]{:S(2)}, u32[]{:S(2)}) collective-permute-start(bf16[16,1280]{1,0:T(8,128)(2,1)S(1)} %get-tuple-element.19.unit_ref), channel_id=1, source_target_pairs={{0,64},{64,0},{1,65},{65,1},{2,66},{66,2},{3,67},{67,3},{4,68},{68... | collective-permute-start | bytes 122888 | tf_op jit(solution)/shard_map/ppermute | solution.py:230
  77.9 5.1 %collective-permute-start.2 = (f32[16,1152]{1,0:T(8,128)S(1)}, f32[16,1152]{1,0:T(8,128)S(1)}, u32[]{:S(2)}, u32[]{:S(2)}) collective-permute-start(f32[16,1152]{1,0:T(8,128)S(1)} %shard_map.71), channel_id=1, source_target_pairs={{0,64},{64,0},{1,65},{65,1},{2,66},{66,2},{3,67},{67,3},{4,68},{68... | collective-permute-start | bytes 221192 | tf_op jit(solution)/shard_map/ppermute | solution.py:235
  95.9 21.6 %copy-start = (bf16[512,1152]{1,0:T(8,128)(2,1)S(1)}, bf16[512,1152]{1,0:T(8,128)(2,1)}, u32[]{:S(2)}) copy-start(bf16[512,1152]{1,0:T(8,128)(2,1)} %captions_ref.1) | copy-start | bytes 3538948
  95.9 21.6 %copy-start.1 = (bf16[128,1152]{1,0:T(8,128)(2,1)S(1)}, bf16[128,1152]{1,0:T(8,128)(2,1)}, u32[]{:S(2)}) copy-start(bf16[128,1152]{1,0:T(8,128)(2,1)} %w_out_ref.1) | copy-start | bytes 884740
  95.9 21.5 %copy-start.2 = (f32[512,128]{1,0:T(8,128)S(1)}, f32[512,128]{1,0:T(8,128)}, u32[]{:S(2)}) copy-start(f32[512,128]{1,0:T(8,128)} %get-tuple-element.21.pre_ref) | copy-start | bytes 786436
  118.9 7.2 %collective-permute-start.3 = (bf16[16,72,128]{2,1,0:T(8,128)(2,1)S(1)}, bf16[16,72,128]{2,1,0:T(8,128)(2,1)S(1)}, u32[]{:S(2)}, u32[]{:S(2)}) collective-permute-start(bf16[16,72,128]{2,1,0:T(8,128)(2,1)S(1)} %get-tuple-element.23), channel_id=1, source_target_pairs={{0,32},{32,0},{1,33},{33,1},{2,34},{34,2},{3,35},{35,3},{4,36},{36... | collective-permute-start | bytes 884744 | tf_op jit(solution)/shard_map/ppermute | solution.py:261

commit v8 on v7

--- a/solution.py
+++ b/solution.py
@@ -9,6 +9,7 @@
 from jax.sharding import Mesh
 from jax.sharding import PartitionSpec as P
 
+
 DP = ("y", "xl", "core")
 BLK = ("z", "xh")
 CHIPS = ("core", "z", "xh")
@@ -17,6 +18,7 @@
 BIAS = -5.0
 EPS = 1e-06
 DIGIT = 32
+LANES = 128
 CURVE = math.sqrt(2.0 / math.pi)
 CUBIC = 0.044715
 GRANT = 60 * 1024 * 1024
@@ -121,15 +123,17 @@
     return jnp.dot(mismatch, img, preferred_element_type=F32)
 
 
-def norm_kernel(where, sum_ref, pair_ref, dir_ref, norm_ref, unit_ref):
+def norm_kernel(first, sum_ref, pairs_ref, dir_ref, norm_ref, unit_ref):
     embedding = sum_ref[...]
-    width = embedding.shape[1]
+    own, width = embedding.shape
     inv_norm = lax.rsqrt(jnp.sum(embedding * embedding, axis=1, keepdims=True) + EPS)
     unit_dir = embedding * inv_norm
     dir_ref[...] = unit_dir
     norm_ref[...] = jnp.broadcast_to(inv_norm, norm_ref.shape)
-    pair = pair_ref[...]
-    lane = lax.broadcasted_iota(jnp.int32, pair.shape, 1)
+    lane = lax.broadcasted_iota(jnp.int32, (own, LANES), 1)
+    spot = first[0] % LANES + lax.broadcasted_iota(jnp.int32, (own, LANES), 0)
+    line = jnp.broadcast_to(pairs_ref[pl.ds(first[0] // LANES, 1), :], (own, LANES))
+    pair = jnp.sum(jnp.where(lane == spot, line, 0).astype(F32), axis=1, keepdims=True).astype(jnp.int32)
     digits = jnp.where(lane == 0, pair // DIGIT, jnp.where(lane == 1, pair % DIGIT, 0))
     unit_ref[:, :width] = unit_dir.astype(BF16)
     unit_ref[:, width:] = digits.astype(F32).astype(BF16)
@@ -209,25 +213,25 @@
     img = got[:, per_first:].reshape(n_xh * img_part, width).astype(F32)
     img = (img * lax.rsqrt(jnp.sum(img * img, axis=1, keepdims=True) + EPS)).astype(BF16)
     sent = jnp.concatenate([partial.reshape(n_z, own, width), to_all(img, n_z)], axis=1)
+    at_first, at_second = place(core, n_z, n_xh, lax.axis_index("z"), lax.axis_index("xh"))
+    begin = (at_first * per_first + at_second * own).reshape(1).astype(jnp.int32)
+    sent, begin = lax.optimization_barrier((sent, begin))
     got = exchange(sent, CHIPS, second)
     embedding = jnp.sum(got[:, :own].astype(F32), axis=0)
     embedding, img = lax.optimization_barrier((embedding, got[:, own:].reshape(-1, width)))
 
-    at_first, at_second = place(core, n_z, n_xh, lax.axis_index("z"), lax.axis_index("xh"))
-    pair = lax.dynamic_slice_in_dim(pairs, at_first * per_first + at_second * own, own, 0)
-    pair = jnp.broadcast_to(pair[:, None], (own, 128))
     row = jax.ShapeDtypeStruct((own, width), F32)
     unit_dir, inv_norm, unit = call(
         norm_kernel,
-        (row, jax.ShapeDtypeStruct((own, 128), F32), jax.ShapeDtypeStruct((own, width + 128), BF16)),
+        (row, jax.ShapeDtypeStruct((own, LANES), F32), jax.ShapeDtypeStruct((own, width + LANES), BF16)),
         own * width,
-        here,
+        begin,
         embedding,
-        pair,
+        pairs.reshape(-1, LANES),
     )
     unit, img = lax.optimization_barrier((unit, img))
+    other_unit = lax.ppermute(unit, "xl", swap)
     other_img = lax.ppermute(img, "core", swap)
-    other_unit = lax.ppermute(unit, "xl", swap)
     score = functools.partial(score_kernel, (n_z, n_xh, img_block, img_part))
     flops = 8 * own * img.shape[0] * width
     grad = call(score, row, flops, here, unit, img, other_img)

time: 146 us -> 145 us (level)
  starting transfers between devices: 27.4 us -> 34.2 us
  blocking collectives: 89 us -> 82.2 us
    all_to_all x1, starting transfers between devices: 6.68 us -> 16.3 us  [exchange(): return lax.all_to_all(x, axes, 0, 0, axis_index_groups=groups, tiled=True)]
    all_to_all x4, blocking collectives: 89 us -> 82.2 us  [exchange(): return lax.all_to_all(x, axes, 0, 0, axis_index_groups=groups, tiled=True)]
    ppermute x1, starting transfers between devices: 3.46 us -> 1.92 us  [body(): other_unit = lax.ppermute(unit, 'xl', swap)]
  transfers between devices with their start and end apart: 5 -> 5, of which waited for: 4 -> 4; matrix products, arithmetic and copies ran while one was open for 1% -> 0% of each run, Pallas kernels for 0% -> 0%
where the time goes in v8:
time: 145 us
  blocking collectives  82.2 us (57%)
  starting transfers between devices  34.2 us (24%)
  waiting for transfers between devices  19.6 us (14%)
  Pallas kernels  6.45 us (4%)
    all_to_all x4, blocking collectives, exchange(): return lax.all_to_all(x, axes, 0, 0, axis_index_groups=groups, tiled=True)  82.2 us
    all_to_all x1, starting transfers between devices, exchange(): return lax.all_to_all(x, axes, 0, 0, axis_index_groups=groups, tiled=True)  16.3 us
    all_to_all x1, waiting for transfers between devices, exchange(): return lax.all_to_all(x, axes, 0, 0, axis_index_groups=groups, tiled=True)  13.7 us
    ppermute x1, starting transfers between devices, body(): other_img = lax.ppermute(img, 'core', swap)  7.3 us
    pallas_call x6, Pallas kernels, call(): pl.pallas_call(kernel, out_shape=outs, in_specs=[pl.BlockSpec(memory_spac...  6.45 us
    ppermute x1, starting transfers between devices, body(): mine = mine + lax.ppermute(other, 'core', swap).astype(F32)  6.2 us
  transfers between devices with their start and end apart: 5, of which 4 were waited for; matrix products, arithmetic and copies ran while one was open for 0% of the time, Pallas kernels for 0%

profile of v8, /device:TPU:1, one launch (start us, length us, event | category | flops | bytes accessed | tf_op | source)
XLA Modules:
  0.0 144.7 jit_solution(11291155537518800229)
XLA Ops:
  0.6 3.4 %shard_map.68 = (bf16[4,136,1152]{2,1,0:T(8,128)(2,1)}, f32[512,128]{1,0:T(8,128)}) custom-call(s32[1]{0:T(128)} %bitcast.where, bf16[512,1152]{1,0:T(8,128)(2,1)} %captions_ref.1, bf16[1152,128]{1,0:T(8,128)(2,1)} %w_in_hbm.1, bf16[128,1152]{1,0:T(8,128)(2,1)} %w_out_ref.1, bf16[32,1152]{1,0:T(8,128)(2,1)} %images_hbm.1), custom_call_target="tpu_custom_call" | custom-call | flops 301989888 | bytes 3000000 | tf_op jit(solution)/shard_map/pallas_call | solution.py:164
  4.0 16.3 %all-to-all-start = ((bf16[4,136,1152]{2,1,0:T(8,128)(2,1)}), bf16[4,136,1152]{2,1,0:T(8,128)(2,1)S(1)}, u32[]{:S(2)}, u32[]{:S(2)}) async-start(bf16[4,136,1152]{2,1,0:T(8,128)(2,1)} %get-tuple-element.15), calls=%async_computation | async-start | bytes 2506752 | tf_op jit(solution)/shard_map/all_to_all | solution.py:30
  20.4 13.7 %all-to-all-done = bf16[4,136,1152]{2,1,0:T(8,128)(2,1)S(1)} async-done(((bf16[4,136,1152]{2,1,0:T(8,128)(2,1)}), bf16[4,136,1152]{2,1,0:T(8,128)(2,1)S(1)}, u32[]{:S(2)}, u32[]{:S(2)}) %all-to-all-start) | async-done | bytes 1253408 | tf_op jit(solution)/shard_map/all_to_all | solution.py:30
  34.0 0.1 fusion.2
  34.1 0.1 rsqrt.12
  34.2 0.2 slice_reduce_fusion
  34.4 0.1 fusion.1
  34.5 0.1 pad_maximum_fusion
  34.6 0.0 copy-start.3
  34.6 28.6 %all_to_all.25 = bf16[8,48,1152]{2,1,0:T(8,128)(2,1)S(1)} all-to-all(bf16[8,48,1152]{2,1,0:T(8,128)(2,1)S(1)} %pad_maximum_fusion), channel_id=1, replica_groups={{0,4,8,12,16,20,24,28},{1,5,9,13,17,21,25,29},{2,6,10,14,18,22,26,30},{..., dimensions={0} | all-to-all | bytes 1769472 | tf_op jit(solution)/shard_map/all_to_all | solution.py:30
  63.3 0.1 shard_map.69
  63.4 7.3 %collective-permute-start = (bf16[256,1152]{1,0:T(8,128)(2,1)S(1)}, bf16[256,1152]{1,0:T(8,128)(2,1)S(1)}, u32[]{:S(2)}, u32[]{:S(2)}) collective-permute-start(bf16[256,1152]{1,0:T(8,128)(2,1)S(1)} %bitcast.13), channel_id=1, source_target_pairs={{0,32},{32,0},{1,33},{33,1},{2,34},{34,2},{3,35},{35,3},{4,36},{36... | collective-permute-start | bytes 1769480 | tf_op jit(solution)/shard_map/ppermute | solution.py:234
  70.7 1.9 %collective-permute-start.1 = (bf16[16,1280]{1,0:T(8,128)(2,1)S(1)}, bf16[16,1280]{1,0:T(8,128)(2,1)S(1)}, u32[]{:S(2)}, u32[]{:S(2)}) collective-permute-start(bf16[16,1280]{1,0:T(8,128)(2,1)S(1)} %get-tuple-element.23.unit_ref), channel_id=1, source_target_pairs={{0,64},{64,0},{1,65},{65,1},{2,66},{66,2},{3,67},{67,3},{4,68},{68... | collective-permute-start | bytes 122888 | tf_op jit(solution)/shard_map/ppermute | solution.py:233
  72.6 2.8 %collective-permute-done.1.unit_ref = bf16[16,1280]{1,0:T(8,128)(2,1)S(1)} collective-permute-done((bf16[16,1280]{1,0:T(8,128)(2,1)S(1)}, bf16[16,1280]{1,0:T(8,128)(2,1)S(1)}, u32[]{:S(2)}, u32[]{:S(2)}) %collective-permute-start.1) | collective-permute-done | bytes 40992 | tf_op jit(solution)/shard_map/ppermute | solution.py:233
  75.4 0.0 collective-permute-done.other_ref
  75.4 0.7 shard_map.71
  76.1 2.5 %collective-permute-start.2 = (f32[16,1152]{1,0:T(8,128)S(1)}, f32[16,1152]{1,0:T(8,128)S(1)}, u32[]{:S(2)}, u32[]{:S(2)}) collective-permute-start(f32[16,1152]{1,0:T(8,128)S(1)} %shard_map.71), channel_id=1, source_target_pairs={{0,64},{64,0},{1,65},{65,1},{2,66},{66,2},{3,67},{67,3},{4,68},{68... | collective-permute-start | bytes 221192 | tf_op jit(solution)/shard_map/ppermute | solution.py:239
  78.6 0.7 shard_map.70.mine_ref
  79.2 2.0 %collective-permute-done.2.other_ref = f32[16,1152]{1,0:T(8,128)S(1)} collective-permute-done((f32[16,1152]{1,0:T(8,128)S(1)}, f32[16,1152]{1,0:T(8,128)S(1)}, u32[]{:S(2)}, u32[]{:S(2)}) %collective-permute-start.2) | collective-permute-done | bytes 73760 | tf_op jit(solution)/shard_map/ppermute | solution.py:239
  81.2 0.1 shard_map.72
  81.3 12.8 %all_to_all.26 = bf16[8,16,1152]{2,1,0:T(8,128)(2,1)S(1)} all-to-all(bf16[8,16,1152]{2,1,0:T(8,128)(2,1)S(1)} %shard_map.72), channel_id=1, replica_groups={{0,4,8,12,16,20,24,28},{1,5,9,13,17,21,25,29},{2,6,10,14,18,22,26,30},{..., dimensions={0} | all-to-all | bytes 589824 | tf_op jit(solution)/shard_map/all_to_all | solution.py:30
  94.2 0.1 broadcast_in_dim.16
  94.3 0.0 copy-start
  94.3 0.0 copy-start.1
  94.3 22.8 %all_to_all.27 = bf16[4,128,1152]{2,1,0:T(8,128)(2,1)S(1)} all-to-all(bf16[4,128,1152]{2,1,0:T(8,128)(2,1)S(1)} %broadcast_in_dim.16), channel_id=1, replica_groups={{0,1,2,3},{4,5,6,7},{8,9,10,11},{12,13,14,15},{16,17,18,19},{20,21,22,2..., dimensions={0} | all-to-all | bytes 2359296 | tf_op jit(solution)/shard_map/all_to_all | solution.py:30
  117.1 0.0 copy-done.1
  117.1 1.5 %shard_map.73 = (f32[16,72,128]{2,1,0:T(8,128)S(1)}, bf16[16,72,128]{2,1,0:T(8,128)(2,1)S(1)}) custom-call(s32[1]{0:T(128)} %bitcast.where, bf16[512,1152]{1,0:T(8,128)(2,1)S(1)} %copy-done, bf16[512,1152]{1,0:T(8,128)(2,1)S(1)} %bitcast.16, bf16[128,1152]{1,0:T(8,128)(2,1)S(1)} %copy-done.1, f32[512,128]{1,0:T(8,128)S(1)} %copy-done.2), custom_call_target="tpu_custom_call" | custom-call | flops 452984832 | bytes 3000000 | tf_op jit(solution)/shard_map/pallas_call | solution.py:164
  118.6 6.2 %collective-permute-start.3 = (bf16[16,72,128]{2,1,0:T(8,128)(2,1)S(1)}, bf16[16,72,128]{2,1,0:T(8,128)(2,1)S(1)}, u32[]{:S(2)}, u32[]{:S(2)}) collective-permute-start(bf16[16,72,128]{2,1,0:T(8,128)(2,1)S(1)} %get-tuple-element.27), channel_id=1, source_target_pairs={{0,32},{32,0},{1,33},{33,1},{2,34},{34,2},{3,35},{35,3},{4,36},{36... | collective-permute-start | bytes 884744 | tf_op jit(solution)/shard_map/ppermute | solution.py:265
  124.8 1.2 collective-permute-done.3
  126.0 0.1 add_convert_fusion
  126.0 18.0 %all_to_all.28 = bf16[16,72,128]{2,1,0:T(8,128)(2,1)S(1)} all-to-all(bf16[16,72,128]{2,1,0:T(8,128)(2,1)S(1)} %add_convert_fusion), channel_id=1, replica_groups=mesh['y'=8,'xl'=2,'core'=2,'z'=8,'xh'=4] {'y','xl'}, dimensions={0} | all-to-all | bytes 589824 | tf_op jit(solution)/shard_map/all_to_all | solution.py:30
  144.1 0.6 fusion.3
  (9 shorter events, 0.2 us)
Async XLA Ops:
  4.0 30.0 %all-to-all-start = ((bf16[4,136,1152]{2,1,0:T(8,128)(2,1)}), bf16[4,136,1152]{2,1,0:T(8,128)(2,1)S(1)}, u32[]{:S(2)}, u32[]{:S(2)}) async-start(bf16[4,136,1152]{2,1,0:T(8,128)(2,1)} %get-tuple-element.15), calls=%async_computation | async-start | bytes 2506752 | tf_op jit(solution)/shard_map/all_to_all | solution.py:30
  34.6 28.7 %copy-start.3 = (s32[512]{0:T(512)S(1)}, s32[512]{0:T(512)}, u32[]{:S(2)}) copy-start(s32[512]{0:T(512)} %param.9) | copy-start | bytes 6148
  63.4 12.1 %collective-permute-start = (bf16[256,1152]{1,0:T(8,128)(2,1)S(1)}, bf16[256,1152]{1,0:T(8,128)(2,1)S(1)}, u32[]{:S(2)}, u32[]{:S(2)}) collective-permute-start(bf16[256,1152]{1,0:T(8,128)(2,1)S(1)} %bitcast.13), channel_id=1, source_target_pairs={{0,32},{32,0},{1,33},{33,1},{2,34},{34,2},{3,35},{35,3},{4,36},{36... | collective-permute-start | bytes 1769480 | tf_op jit(solution)/shard_map/ppermute | solution.py:234
  70.7 4.7 %collective-permute-start.1 = (bf16[16,1280]{1,0:T(8,128)(2,1)S(1)}, bf16[16,1280]{1,0:T(8,128)(2,1)S(1)}, u32[]{:S(2)}, u32[]{:S(2)}) collective-permute-start(bf16[16,1280]{1,0:T(8,128)(2,1)S(1)} %get-tuple-element.23.unit_ref), channel_id=1, source_target_pairs={{0,64},{64,0},{1,65},{65,1},{2,66},{66,2},{3,67},{67,3},{4,68},{68... | collective-permute-start | bytes 122888 | tf_op jit(solution)/shard_map/ppermute | solution.py:233
  76.1 5.1 %collective-permute-start.2 = (f32[16,1152]{1,0:T(8,128)S(1)}, f32[16,1152]{1,0:T(8,128)S(1)}, u32[]{:S(2)}, u32[]{:S(2)}) collective-permute-start(f32[16,1152]{1,0:T(8,128)S(1)} %shard_map.71), channel_id=1, source_target_pairs={{0,64},{64,0},{1,65},{65,1},{2,66},{66,2},{3,67},{67,3},{4,68},{68... | collective-permute-start | bytes 221192 | tf_op jit(solution)/shard_map/ppermute | solution.py:239
  94.3 22.8 %copy-start = (bf16[512,1152]{1,0:T(8,128)(2,1)S(1)}, bf16[512,1152]{1,0:T(8,128)(2,1)}, u32[]{:S(2)}) copy-start(bf16[512,1152]{1,0:T(8,128)(2,1)} %captions_ref.1) | copy-start | bytes 3538948
  94.3 22.8 %copy-start.1 = (bf16[128,1152]{1,0:T(8,128)(2,1)S(1)}, bf16[128,1152]{1,0:T(8,128)(2,1)}, u32[]{:S(2)}) copy-start(bf16[128,1152]{1,0:T(8,128)(2,1)} %w_out_ref.1) | copy-start | bytes 884740
  94.3 22.8 %copy-start.2 = (f32[512,128]{1,0:T(8,128)S(1)}, f32[512,128]{1,0:T(8,128)}, u32[]{:S(2)}) copy-start(f32[512,128]{1,0:T(8,128)} %get-tuple-element.25.pre_ref) | copy-start | bytes 786436
  118.6 7.4 %collective-permute-start.3 = (bf16[16,72,128]{2,1,0:T(8,128)(2,1)S(1)}, bf16[16,72,128]{2,1,0:T(8,128)(2,1)S(1)}, u32[]{:S(2)}, u32[]{:S(2)}) collective-permute-start(bf16[16,72,128]{2,1,0:T(8,128)(2,1)S(1)} %get-tuple-element.27), channel_id=1, source_target_pairs={{0,32},{32,0},{1,33},{33,1},{2,34},{34,2},{3,35},{35,3},{4,36},{36... | collective-permute-start | bytes 884744 | tf_op jit(solution)/shard_map/ppermute | solution.py:265

commit v9 on v8

--- a/solution.py
+++ b/solution.py
@@ -67,9 +67,12 @@
     fetches = [
         pltpu.make_async_copy(captions_hbm.at[at], captions_ref.at[at], sems.at[3 + k]) for k, at in enumerate(blocks)
     ]
-    for copy in (fetch_in, fetches[0], fetch_out, fetch_img, fetches[1]):
+    for copy in (fetch_img, fetch_in, fetches[0], fetch_out, fetches[1]):
         copy.start()
     stores = []
+    fetch_img.wait()
+    img = img_ref[...].astype(F32)
+    img = (img * lax.rsqrt(jnp.sum(img * img, axis=1, keepdims=True) + EPS)).astype(BF16)
     fetch_in.wait()
     for k, at in enumerate(blocks):
         fetches[k].wait()
@@ -78,11 +81,10 @@
         hidden = (0.5 * pre_act * (1.0 + bend(pre_act))).astype(BF16)
         if k == 0:
             fetch_out.wait()
-            fetch_img.wait()
         total = jnp.dot(hidden, w_out_ref[...], preferred_element_type=F32).astype(BF16)
         for q in range(n):
             out_ref[k * n + q, :per_first] = total[q * per_first : (q + 1) * per_first]
-            out_ref[k * n + q, per_first:] = img_ref[...]
+            out_ref[k * n + q, per_first:] = img
         to = pl.ds(k * n, n)
         stores.append(pltpu.make_async_copy(out_ref.at[to], out_hbm.at[to], sems.at[5 + k]))
         stores.append(pltpu.make_async_copy(pre_ref.at[at], pre_hbm.at[at], sems.at[7 + k]))
@@ -210,8 +212,7 @@
     )
     got = exchange(sent, CHIPS, first)
     partial = jnp.sum(got[:, :per_first].astype(F32), axis=0).astype(BF16)
-    img = got[:, per_first:].reshape(n_xh * img_part, width).astype(F32)
-    img = (img * lax.rsqrt(jnp.sum(img * img, axis=1, keepdims=True) + EPS)).astype(BF16)
+    img = got[:, per_first:].reshape(n_xh * img_part, width)
     sent = jnp.concatenate([partial.reshape(n_z, own, width), to_all(img, n_z)], axis=1)
     at_first, at_second = place(core, n_z, n_xh, lax.axis_index("z"), lax.axis_index("xh"))
     begin = (at_first * per_first + at_second * own).reshape(1).astype(jnp.int32)

time: 145 us -> 145 us (level)
  no operation moved by 1% of the time
where the time goes in v9:
time: 145 us; the launch traced here: 144 us
  blocking collectives  82.2 us (57%)
  starting transfers between devices  34.1 us (24%)
  waiting for transfers between devices  19.6 us (14%)
  Pallas kernels  6.45 us (4%)
    all_to_all x4, blocking collectives, exchange(): return lax.all_to_all(x, axes, 0, 0, axis_index_groups=groups, tiled=True)  82.2 us
    all_to_all x1, starting transfers between devices, exchange(): return lax.all_to_all(x, axes, 0, 0, axis_index_groups=groups, tiled=True)  16.3 us
    all_to_all x1, waiting for transfers between devices, exchange(): return lax.all_to_all(x, axes, 0, 0, axis_index_groups=groups, tiled=True)  13.7 us
    ppermute x1, starting transfers between devices, body(): other_img = lax.ppermute(img, 'core', swap)  7.27 us
    pallas_call x6, Pallas kernels, call(): pl.pallas_call(kernel, out_shape=outs, in_specs=[pl.BlockSpec(memory_spac...  6.45 us
    ppermute x1, starting transfers between devices, body(): mine = mine + lax.ppermute(other, 'core', swap).astype(F32)  6.19 us
  transfers between devices with their start and end apart: 5, of which 4 were waited for; matrix products, arithmetic and copies ran while one was open for 0% of the time, Pallas kernels for 0%

profile of v9, /device:TPU:1, one launch (start us, length us, event | category | flops | bytes accessed | tf_op | source)
XLA Modules:
  0.0 144.4 jit_solution(11063007238676473885)
XLA Ops:
  0.6 3.4 %shard_map.68 = (bf16[4,136,1152]{2,1,0:T(8,128)(2,1)}, f32[512,128]{1,0:T(8,128)}) custom-call(s32[1]{0:T(128)} %bitcast.where, bf16[512,1152]{1,0:T(8,128)(2,1)} %captions_ref.1, bf16[1152,128]{1,0:T(8,128)(2,1)} %w_in_hbm.1, bf16[128,1152]{1,0:T(8,128)(2,1)} %w_out_ref.1, bf16[32,1152]{1,0:T(8,128)(2,1)} %images_hbm.1), custom_call_target="tpu_custom_call" | custom-call | flops 301989888 | bytes 3000000 | tf_op jit(solution)/shard_map/pallas_call | solution.py:166
  4.0 16.3 %all-to-all-start = ((bf16[4,136,1152]{2,1,0:T(8,128)(2,1)}), bf16[4,136,1152]{2,1,0:T(8,128)(2,1)S(1)}, u32[]{:S(2)}, u32[]{:S(2)}) async-start(bf16[4,136,1152]{2,1,0:T(8,128)(2,1)} %get-tuple-element.15), calls=%async_computation | async-start | bytes 2506752 | tf_op jit(solution)/shard_map/all_to_all | solution.py:30
  20.3 13.7 %all-to-all-done = bf16[4,136,1152]{2,1,0:T(8,128)(2,1)S(1)} async-done(((bf16[4,136,1152]{2,1,0:T(8,128)(2,1)}), bf16[4,136,1152]{2,1,0:T(8,128)(2,1)S(1)}, u32[]{:S(2)}, u32[]{:S(2)}) %all-to-all-start) | async-done | bytes 1253408 | tf_op jit(solution)/shard_map/all_to_all | solution.py:30
  34.0 0.2 slice_reduce_fusion
  34.2 0.1 pad_maximum_fusion
  34.3 0.0 copy-start.3
  34.3 28.6 %all_to_all.25 = bf16[8,48,1152]{2,1,0:T(8,128)(2,1)S(1)} all-to-all(bf16[8,48,1152]{2,1,0:T(8,128)(2,1)S(1)} %pad_maximum_fusion), channel_id=1, replica_groups={{0,4,8,12,16,20,24,28},{1,5,9,13,17,21,25,29},{2,6,10,14,18,22,26,30},{..., dimensions={0} | all-to-all | bytes 1769472 | tf_op jit(solution)/shard_map/all_to_all | solution.py:30
  63.0 0.0 copy-done.3
  63.0 0.1 shard_map.69
  63.1 7.3 %collective-permute-start = (bf16[256,1152]{1,0:T(8,128)(2,1)S(1)}, bf16[256,1152]{1,0:T(8,128)(2,1)S(1)}, u32[]{:S(2)}, u32[]{:S(2)}) collective-permute-start(bf16[256,1152]{1,0:T(8,128)(2,1)S(1)} %bitcast.9), channel_id=1, source_target_pairs={{0,32},{32,0},{1,33},{33,1},{2,34},{34,2},{3,35},{35,3},{4,36},{36... | collective-permute-start | bytes 1769480 | tf_op jit(solution)/shard_map/ppermute | solution.py:235
  70.4 1.9 %collective-permute-start.1 = (bf16[16,1280]{1,0:T(8,128)(2,1)S(1)}, bf16[16,1280]{1,0:T(8,128)(2,1)S(1)}, u32[]{:S(2)}, u32[]{:S(2)}) collective-permute-start(bf16[16,1280]{1,0:T(8,128)(2,1)S(1)} %get-tuple-element.23.unit_ref), channel_id=1, source_target_pairs={{0,64},{64,0},{1,65},{65,1},{2,66},{66,2},{3,67},{67,3},{4,68},{68... | collective-permute-start | bytes 122888 | tf_op jit(solution)/shard_map/ppermute | solution.py:234
  72.3 2.8 %collective-permute-done.1.unit_ref = bf16[16,1280]{1,0:T(8,128)(2,1)S(1)} collective-permute-done((bf16[16,1280]{1,0:T(8,128)(2,1)S(1)}, bf16[16,1280]{1,0:T(8,128)(2,1)S(1)}, u32[]{:S(2)}, u32[]{:S(2)}) %collective-permute-start.1) | collective-permute-done | bytes 40992 | tf_op jit(solution)/shard_map/ppermute | solution.py:234
  75.1 0.0 collective-permute-done.other_ref
  75.1 0.7 shard_map.71
  75.8 2.5 %collective-permute-start.2 = (f32[16,1152]{1,0:T(8,128)S(1)}, f32[16,1152]{1,0:T(8,128)S(1)}, u32[]{:S(2)}, u32[]{:S(2)}) collective-permute-start(f32[16,1152]{1,0:T(8,128)S(1)} %shard_map.71), channel_id=1, source_target_pairs={{0,64},{64,0},{1,65},{65,1},{2,66},{66,2},{3,67},{67,3},{4,68},{68... | collective-permute-start | bytes 221192 | tf_op jit(solution)/shard_map/ppermute | solution.py:240
  78.3 0.7 shard_map.70.mine_ref
  79.0 2.0 %collective-permute-done.2.other_ref = f32[16,1152]{1,0:T(8,128)S(1)} collective-permute-done((f32[16,1152]{1,0:T(8,128)S(1)}, f32[16,1152]{1,0:T(8,128)S(1)}, u32[]{:S(2)}, u32[]{:S(2)}) %collective-permute-start.2) | collective-permute-done | bytes 73760 | tf_op jit(solution)/shard_map/ppermute | solution.py:240
  80.9 0.1 shard_map.72
  81.0 12.8 %all_to_all.26 = bf16[8,16,1152]{2,1,0:T(8,128)(2,1)S(1)} all-to-all(bf16[8,16,1152]{2,1,0:T(8,128)(2,1)S(1)} %shard_map.72), channel_id=1, replica_groups={{0,4,8,12,16,20,24,28},{1,5,9,13,17,21,25,29},{2,6,10,14,18,22,26,30},{..., dimensions={0} | all-to-all | bytes 589824 | tf_op jit(solution)/shard_map/all_to_all | solution.py:30
  93.9 0.1 broadcast_in_dim.17
  94.0 0.0 copy-start
  94.0 0.0 copy-start.1
  94.0 0.0 copy-start.2
  94.0 22.8 %all_to_all.27 = bf16[4,128,1152]{2,1,0:T(8,128)(2,1)S(1)} all-to-all(bf16[4,128,1152]{2,1,0:T(8,128)(2,1)S(1)} %broadcast_in_dim.17), channel_id=1, replica_groups={{0,1,2,3},{4,5,6,7},{8,9,10,11},{12,13,14,15},{16,17,18,19},{20,21,22,2..., dimensions={0} | all-to-all | bytes 2359296 | tf_op jit(solution)/shard_map/all_to_all | solution.py:30
  116.8 0.0 copy-done
  116.8 0.0 copy-done.1
  116.8 1.5 %shard_map.73 = (f32[16,72,128]{2,1,0:T(8,128)S(1)}, bf16[16,72,128]{2,1,0:T(8,128)(2,1)S(1)}) custom-call(s32[1]{0:T(128)} %bitcast.where, bf16[512,1152]{1,0:T(8,128)(2,1)S(1)} %copy-done, bf16[512,1152]{1,0:T(8,128)(2,1)S(1)} %bitcast.12, bf16[128,1152]{1,0:T(8,128)(2,1)S(1)} %copy-done.1, f32[512,128]{1,0:T(8,128)S(1)} %copy-done.2), custom_call_target="tpu_custom_call" | custom-call | flops 452984832 | bytes 3000000 | tf_op jit(solution)/shard_map/pallas_call | solution.py:166
  118.3 6.2 %collective-permute-start.3 = (bf16[16,72,128]{2,1,0:T(8,128)(2,1)S(1)}, bf16[16,72,128]{2,1,0:T(8,128)(2,1)S(1)}, u32[]{:S(2)}, u32[]{:S(2)}) collective-permute-start(bf16[16,72,128]{2,1,0:T(8,128)(2,1)S(1)} %get-tuple-element.27), channel_id=1, source_target_pairs={{0,32},{32,0},{1,33},{33,1},{2,34},{34,2},{3,35},{35,3},{4,36},{36... | collective-permute-start | bytes 884744 | tf_op jit(solution)/shard_map/ppermute | solution.py:266
  124.5 1.2 collective-permute-done.3
  125.7 0.1 add_convert_fusion
  125.7 18.0 %all_to_all.28 = bf16[16,72,128]{2,1,0:T(8,128)(2,1)S(1)} all-to-all(bf16[16,72,128]{2,1,0:T(8,128)(2,1)S(1)} %add_convert_fusion), channel_id=1, replica_groups=mesh['y'=8,'xl'=2,'core'=2,'z'=8,'xh'=4] {'y','xl'}, dimensions={0} | all-to-all | bytes 589824 | tf_op jit(solution)/shard_map/all_to_all | solution.py:30
  143.8 0.6 fusion
  (6 shorter events, 0.2 us)
Async XLA Ops:
  4.0 30.0 %all-to-all-start = ((bf16[4,136,1152]{2,1,0:T(8,128)(2,1)}), bf16[4,136,1152]{2,1,0:T(8,128)(2,1)S(1)}, u32[]{:S(2)}, u32[]{:S(2)}) async-start(bf16[4,136,1152]{2,1,0:T(8,128)(2,1)} %get-tuple-element.15), calls=%async_computation | async-start | bytes 2506752 | tf_op jit(solution)/shard_map/all_to_all | solution.py:30
  34.3 28.7 %copy-start.3 = (s32[512]{0:T(512)S(1)}, s32[512]{0:T(512)}, u32[]{:S(2)}) copy-start(s32[512]{0:T(512)} %param.9) | copy-start | bytes 6148
  63.1 12.0 %collective-permute-start = (bf16[256,1152]{1,0:T(8,128)(2,1)S(1)}, bf16[256,1152]{1,0:T(8,128)(2,1)S(1)}, u32[]{:S(2)}, u32[]{:S(2)}) collective-permute-start(bf16[256,1152]{1,0:T(8,128)(2,1)S(1)} %bitcast.9), channel_id=1, source_target_pairs={{0,32},{32,0},{1,33},{33,1},{2,34},{34,2},{3,35},{35,3},{4,36},{36... | collective-permute-start | bytes 1769480 | tf_op jit(solution)/shard_map/ppermute | solution.py:235
  70.4 4.7 %collective-permute-start.1 = (bf16[16,1280]{1,0:T(8,128)(2,1)S(1)}, bf16[16,1280]{1,0:T(8,128)(2,1)S(1)}, u32[]{:S(2)}, u32[]{:S(2)}) collective-permute-start(bf16[16,1280]{1,0:T(8,128)(2,1)S(1)} %get-tuple-element.23.unit_ref), channel_id=1, source_target_pairs={{0,64},{64,0},{1,65},{65,1},{2,66},{66,2},{3,67},{67,3},{4,68},{68... | collective-permute-start | bytes 122888 | tf_op jit(solution)/shard_map/ppermute | solution.py:234
  75.8 5.1 %collective-permute-start.2 = (f32[16,1152]{1,0:T(8,128)S(1)}, f32[16,1152]{1,0:T(8,128)S(1)}, u32[]{:S(2)}, u32[]{:S(2)}) collective-permute-start(f32[16,1152]{1,0:T(8,128)S(1)} %shard_map.71), channel_id=1, source_target_pairs={{0,64},{64,0},{1,65},{65,1},{2,66},{66,2},{3,67},{67,3},{4,68},{68... | collective-permute-start | bytes 221192 | tf_op jit(solution)/shard_map/ppermute | solution.py:240
  94.0 22.8 %copy-start = (bf16[512,1152]{1,0:T(8,128)(2,1)S(1)}, bf16[512,1152]{1,0:T(8,128)(2,1)}, u32[]{:S(2)}) copy-start(bf16[512,1152]{1,0:T(8,128)(2,1)} %captions_ref.1) | copy-start | bytes 3538948
  94.0 22.8 %copy-start.1 = (bf16[128,1152]{1,0:T(8,128)(2,1)S(1)}, bf16[128,1152]{1,0:T(8,128)(2,1)}, u32[]{:S(2)}) copy-start(bf16[128,1152]{1,0:T(8,128)(2,1)} %w_out_ref.1) | copy-start | bytes 884740
  94.0 22.8 %copy-start.2 = (f32[512,128]{1,0:T(8,128)S(1)}, f32[512,128]{1,0:T(8,128)}, u32[]{:S(2)}) copy-start(f32[512,128]{1,0:T(8,128)} %get-tuple-element.25.pre_ref) | copy-start | bytes 786436
  118.3 7.4 %collective-permute-start.3 = (bf16[16,72,128]{2,1,0:T(8,128)(2,1)S(1)}, bf16[16,72,128]{2,1,0:T(8,128)(2,1)S(1)}, u32[]{:S(2)}, u32[]{:S(2)}) collective-permute-start(bf16[16,72,128]{2,1,0:T(8,128)(2,1)S(1)} %get-tuple-element.27), channel_id=1, source_target_pairs={{0,32},{32,0},{1,33},{33,1},{2,34},{34,2},{3,35},{35,3},{4,36},{36... | collective-permute-start | bytes 884744 | tf_op jit(solution)/shard_map/ppermute | solution.py:266
